TPU v7x, 32 devices: a whole 2x2x4 slice. The times are simulated.
32 devices in a mesh: lat: 8 (over z, y), wall: 4 (over x, core).
Axes of the slice: x: 2, y: 2, z: 4, core: 2. Of those that a mesh axis runs over, the one named last changes fastest.
Arguments:
- populations: float32 [19, 128, 32, 128], P(None, 'wall', 'lat'), may hold values from 0.0138 to 0.5, as said below
- concentration: float32 [128, 4, 32, 128], P('wall', None, 'lat'), may hold values from 0.2 to 2
- cell_flags: int32 [128, 32, 128], P('wall', 'lat'), may hold values from 0 to 2, as said below
- valence: int32 [4], replicated, may hold values from -2 to 2, as said below
- diffusivity: float32 [4], replicated, may hold values from 1000 to 4000
- applied_field: float32 [3], replicated, may hold values from -1 to 1
Outputs:
- new_populations: float32 [19, 128, 32, 128], P(None, 'wall', 'lat')
- new_concentration: float32 [128, 4, 32, 128], P('wall', None, 'lat')
Inputs may be any that keep to these rules, and one draw needn't show every extreme that they name: `populations`: each population is its lattice weight times a factor between 0.5 and 1.5. `cell_flags`: cells at the first and last wall-normal index and at the first and last index of the split lateral dimension are 1; every wall-normal index z with z % 16 == 8 is 2 away from those; other cells are 0 or 1. `valence`: each entry is -2, -1, 1 or 2; two species are positive and two negative, and one species of each sign has magnitude 2.
All inputs are finite; a program needn't handle non-finite values.
Results may differ from a plain program's by a relative error of at most 0.0003.
Values sent between devices are 32-bit elements; how exact they have to be, the bound alone decides.
No kernel may reach another device: no remote copies, remote signals or barrier semaphores. Data moves between devices by JAX's collectives and lax.ppermute only.
A program may use at most 64 MiB of HBM per device.

v0:
```python
import functools

import jax
import jax.numpy as jnp
from jax import lax
from jax.experimental import pallas as pl
from jax.experimental.pallas import tpu as pltpu
from jax.sharding import PartitionSpec as P

lattice_dirs = (
    (0, 0, 0),
    (1, 0, 0),
    (-1, 0, 0),
    (0, 1, 0),
    (0, -1, 0),
    (0, 0, 1),
    (0, 0, -1),
    (1, 1, 0),
    (-1, -1, 0),
    (1, -1, 0),
    (-1, 1, 0),
    (1, 0, 1),
    (-1, 0, -1),
    (1, 0, -1),
    (-1, 0, 1),
    (0, 1, 1),
    (0, -1, -1),
    (0, 1, -1),
    (0, -1, 1),
)
DIRS = len(lattice_dirs)
FORCE_GAIN = 0.02
X_CELLS = 4
SPECIES = 4
LANES = 128
F32 = jnp.float32

x_plus = tuple(q for q in range(DIRS) if lattice_dirs[q][0] == 1)
x_minus = tuple(q for q in range(DIRS) if lattice_dirs[q][0] == -1)
z_plus = tuple(q for q in range(DIRS) if lattice_dirs[q][2] == 1)
z_minus = tuple(q for q in range(DIRS) if lattice_dirs[q][2] == -1)
FACE_ROWS = 24

VMEM_SPEC = pl.BlockSpec(memory_space=pltpu.VMEM)
SMEM_SPEC = pl.BlockSpec(memory_space=pltpu.SMEM)
ANY_SPEC = pl.BlockSpec(memory_space=pl.ANY)


def on_chip(*shape, dtype=F32):
    return pltpu.VMEM(shape, dtype)


def params():
    return pltpu.CompilerParams(vmem_limit_bytes=24 * 1024 * 1024)


def cost(flops, nbytes):
    return pl.CostEstimate(flops=flops, bytes_accessed=nbytes, transcendentals=0)


def pin(*arrays):
    return [pltpu.with_memory_space_constraint(a, pltpu.VMEM) for a in arrays]


def out_even(q):
    step_x, _, step_z = lattice_dirs[q]
    return {0: 12, 1: 16, -1: 8}[step_z] + (0 if step_x > 0 else 3)


def out_odd(q):
    step_x, _, step_z = lattice_dirs[q]
    return {0: 8, 1: 12, -1: 4}[step_z] + (0 if step_x > 0 else 3)


def low_rows():
    return lax.broadcasted_iota(jnp.int32, (8, LANES), 0) < 4


def collide_kernel(
    pops_hbm,
    conc_hbm,
    flags_hbm,
    valence,
    field,
    moved,
    even_msg,
    odd_msg,
    vel_z,
    conc,
    flags,
    pops,
    sems,
    *,
    tiles,
    chunks,
):
    per = tiles // chunks * 8
    copies = []
    flag_copy = pltpu.make_async_copy(flags_hbm, flags, sems.at[0])
    flag_copy.start()
    for c in range(chunks):
        rows = pl.ds(c * per, per)
        crows = pl.ds(c * per * SPECIES, per * SPECIES)
        pair = (
            pltpu.make_async_copy(conc_hbm.at[crows], conc.at[crows], sems.at[1 + 2 * c]),
            pltpu.make_async_copy(pops_hbm.at[:, rows], pops.at[:, rows], sems.at[2 + 2 * c]),
        )
        for copy in pair:
            copy.start()
        copies.append(pair)
    low = low_rows()
    val_pair = [
        jnp.where(low, valence[2 * h].astype(F32), valence[2 * h + 1].astype(F32))
        for h in range(2)
    ]
    field_xyz = [FORCE_GAIN * field[axis] for axis in range(3)]
    zero = jnp.zeros((8, LANES), F32)
    held = {q: zero for q in z_plus + z_minus}
    flag_copy.wait()
    for k in range(tiles):
        if k % (tiles // chunks) == 0:
            for copy in copies[k // (tiles // chunks)]:
                copy.wait()
        p = [pops[q, pl.ds(8 * k, 8)] for q in range(DIRS)]
        solid = flags[pl.ds(8 * k, 8)] != 0
        sums = []
        for z in range(2):
            part = val_pair[0] * conc[pl.ds(32 * k + 16 * z, 8)]
            part = part + val_pair[1] * conc[pl.ds(32 * k + 16 * z + 8, 8)]
            sums.append(part + pltpu.roll(part, 4, axis=0))
        charge = jnp.where(low, sums[0], sums[1])
        force = [charge * f for f in field_xyz]
        diff = {q: p[q] - p[q + 1] for q in range(1, DIRS, 2)}
        total = {q: p[q] + p[q + 1] for q in range(1, DIRS, 2)}
        density = (
            (p[0] + total[1])
            + (total[3] + total[5])
            + (total[7] + total[9])
            + (total[11] + total[13])
            + (total[15] + total[17])
        )
        momentum = [
            (diff[1] + diff[7]) + (diff[9] + diff[11]) + diff[13],
            (diff[3] + diff[7]) - (diff[9] - diff[15]) + diff[17],
            (diff[5] + diff[11]) - (diff[13] - diff[15]) - diff[17],
        ]
        inverse = 1.0 / density
        vel = [(momentum[a] + 0.5 * force[a]) * inverse for a in range(3)]
        vel_z[pl.ds(8 * k, 8)] = vel[2]
        speed_sq = vel[0] * vel[0] + vel[1] * vel[1] + vel[2] * vel[2]
        work = vel[0] * force[0] + vel[1] * force[1] + vel[2] * force[2]
        base = (1.25 * density) * (1.0 - 1.5 * speed_sq) - 1.125 * work
        odd36 = [(3.75 / 36.0) * density * vel[a] + (1.125 / 36.0) * force[a] for a in range(3)]
        even36 = [(5.625 / 36.0) * density * vel[a] + (3.375 / 36.0) * force[a] for a in range(3)]
        base36 = base * (1.0 / 36.0)
        base18 = base * (1.0 / 18.0)
        for q in range(DIRS):
            if q == 0:
                results = [(0, -0.25 * p[0] + base * (1.0 / 3.0), p[0])]
            elif q % 2 == 1:
                axes = [(a, lattice_dirs[q][a]) for a in range(3) if lattice_dirs[q][a]]

                def along(v):
                    out = v[axes[0][0]]
                    for a, sign in axes[1:]:
                        out = out + v[a] if sign > 0 else out - v[a]
                    return out

                cu, odd, even = along(vel), along(odd36), along(even36)
                if len(axes) == 1:
                    shared = base18 + 2.0 * (cu * even)
                    odd = 2.0 * odd
                else:
                    shared = base36 + cu * even
                results = [
                    (q, (shared + odd) - 0.25 * p[q], p[q + 1]),
                    (q + 1, (shared - odd) - 0.25 * p[q + 1], p[q]),
                ]
            else:
                continue
            for d, relaxed, bounced in results:
                step_x, step_y, step_z = lattice_dirs[d]
                value = jnp.where(solid, bounced, relaxed)
                if step_y:
                    value = pltpu.roll(value, step_y % LANES, axis=1)
                shift = (step_x + 4 * step_z) % 8
                if shift:
                    value = pltpu.roll(value, shift, axis=0)
                if step_z == 0:
                    moved[d, pl.ds(8 + 8 * k, 8)] = value
                else:
                    at = 8 + 8 * k if step_z > 0 else 8 * k
                    moved[d, pl.ds(at, 8)] = jnp.where(low, held[d], value)
                    held[d] = value
    for d in z_plus + z_minus:
        at = 8 + 8 * tiles if lattice_dirs[d][2] > 0 else 8 * tiles
        moved[d, pl.ds(at, 8)] = jnp.where(low, held[d], zero)

    def pack(target, dirs):
        for j, q in enumerate(dirs):
            target[pl.ds(2 * tiles * j, tiles)] = moved[q, pl.ds(out_even(q), tiles, stride=8)]
            target[pl.ds(2 * tiles * j + tiles, tiles)] = moved[
                q, pl.ds(out_odd(q), tiles, stride=8)
            ]

    is_odd = lax.rem(lax.axis_index("lat"), 2) == 1

    @pl.when(jnp.logical_not(is_odd))
    def _():
        pack(even_msg, x_plus)
        pack(odd_msg, x_minus)

    @pl.when(is_odd)
    def _():
        pack(even_msg, x_minus)
        pack(odd_msg, x_plus)


def reciprocal(x):
    return 1.0 / x


def eliminate_kernel(
    vel_z, conc, flags, valence, diffusivity, field, offset, edge, link, ends, *, rows
):
    low = low_rows()
    half = rows // 2
    for h in range(2):
        val = jnp.where(low, valence[2 * h].astype(F32), valence[2 * h + 1].astype(F32))
        diff = jnp.where(low, diffusivity[2 * h], diffusivity[2 * h + 1])
        slow = diff * 0.01
        membrane = diff * jnp.where(val > 0, 0.5, 0.02)
        pull = val * field[2]

        def coefficients(z):
            tile = pl.ds(8 * (z // 2), 8)
            vz, flag = vel_z[tile], flags[tile]
            mine = low if z % 2 == 0 else jnp.logical_not(low)
            vz = jnp.where(mine, vz, pltpu.roll(vz, 4, axis=0))
            flag = jnp.where(mine, flag, pltpu.roll(flag, 4, axis=0))
            spread = jnp.where(flag == 0, diff, jnp.where(flag == 1, slow, membrane))
            drift = spread * jnp.tanh(2.0 * vz + pull)
            lower = 0.5 * spread + 0.25 * drift
            upper = 0.5 * spread - 0.25 * drift
            here = conc[pl.ds(16 * z + 8 * h, 8)]
            rhs = here - spread * here
            if z > 0:
                rhs = rhs + lower * conc[pl.ds(16 * (z - 1) + 8 * h, 8)]
            if z < rows - 1:
                rhs = rhs + upper * conc[pl.ds(16 * (z + 1) + 8 * h, 8)]
            return 1.0 + spread, lower, upper, rhs

        state = {}
        for z_up in range(half):
            for side in range(2):
                z = z_up if side == 0 else rows - 1 - z_up
                main, lower, upper, rhs = coefficients(z)
                back, ahead = (lower, upper) if side == 0 else (upper, lower)
                if z_up == 0:
                    r = reciprocal(main)
                    d, e, k = rhs * r, back * r, ahead * r
                    first = (d, e, k)
                else:
                    d, e, k, first = state[side]
                    r = reciprocal(main - back * k)
                    d, e, k = (rhs + back * d) * r, (back * e) * r, ahead * r
                    first = (first[0] + first[2] * d, first[1] + first[2] * e, first[2] * k)
                state[side] = (d, e, k, first)
                at = pl.ds(16 * z + 8 * h, 8)
                offset[at] = d
                edge[at] = e
                link[at] = k
        (d0, e0, k0, first), (d1, e1, k1, last) = state[0], state[1]
        r = reciprocal(1.0 - k0 * k1)
        high = ((d1 + k1 * d0) * r, (k1 * e0) * r, e1 * r)
        below = ((d0 + k0 * d1) * r, e0 * r, (k0 * e1) * r)
        values = (
            conc[pl.ds(8 * h, 8)] + first[0] + first[2] * high[0],
            first[1] + first[2] * high[1],
            first[2] * high[2],
            conc[pl.ds(16 * (rows - 1) + 8 * h, 8)] + last[0] + last[2] * below[0],
            last[2] * below[1],
            last[1] + last[2] * below[2],
        )
        for j, value in enumerate(values):
            ends[pl.ds(16 * j + 8 * h, 8)] = value


def bit(wall, r):
    return lax.rem(lax.div(wall, 2**r), 2)


def read_ends(ref, h, n=6):
    return [ref[pl.ds(16 * j + 8 * h, 8)] for j in range(n)]


def ordered(own, got, is_upper):
    return (
        [jnp.where(is_upper, g, o) for o, g in zip(own, got)],
        [jnp.where(is_upper, o, g) for o, g in zip(own, got)],
    )


def merge(a, b):
    r = reciprocal(1.0 - a[5] * b[1])
    top_a = ((a[3] + a[5] * b[0]) * r, a[4] * r, (a[5] * b[2]) * r)
    low_b = ((b[0] + b[1] * a[3]) * r, (b[1] * a[4]) * r, b[2] * r)
    merged = (
        a[0] + a[2] * low_b[0],
        a[1] + a[2] * low_b[1],
        a[2] * low_b[2],
        b[3] + b[4] * top_a[0],
        b[4] * top_a[1],
        b[5] + b[4] * top_a[2],
    )
    return top_a, low_b, merged


def relay_kernel(*refs, tiles, level, last):
    own, got, moved, even_got, odd_got = refs[:5]
    up_msg = refs[5]
    pair_msg = refs[6] if level == 0 else None
    wall, lat = lax.axis_index("wall"), lax.axis_index("lat")
    lats = lax.axis_size("lat")
    is_upper = bit(wall, level) == 1
    next_upper = bit(wall, level + 1) == 1
    for h in range(2):
        a, b = ordered(read_ends(own, h), read_ends(got, h), is_upper)
        merged = merge(a, b)[2]
        if last:
            send = [
                jnp.where(next_upper, merged[0], merged[3]),
                jnp.where(next_upper, merged[1], merged[5]),
            ]
        else:
            send = merged
        for j, value in enumerate(send):
            up_msg[pl.ds(16 * j + 8 * h, 8)] = value
    base = 32 if last else 96
    odd_lat = lax.rem(lat, 2) == 1
    part = 2 * tiles

    def from_lat(q, odd_z, index):
        dirs = x_plus if q in x_plus else x_minus
        j = dirs.index(q)
        at = pl.ds(part * j + (tiles if odd_z else 0) + index, 1)
        use_even = odd_lat if q in x_plus else jnp.logical_not(odd_lat)
        exists = lat > 0 if q in x_plus else lat < lats - 1
        row = jnp.where(use_even, even_got[at], odd_got[at])
        return jnp.where(exists, row, 0.0)

    def faces(target, start, dirs):
        for j, q in enumerate(dirs):
            up = lattice_dirs[q][2] > 0
            rows = pl.ds(8 * tiles + 8, 4) if up else pl.ds(4, 4)
            target[pl.ds(start + 4 * j, 4)] = moved[q, rows]
            step_x = lattice_dirs[q][0]
            if step_x:
                at = start + 4 * j + (0 if step_x > 0 else 3)
                target[pl.ds(at, 1)] = from_lat(q, up, tiles - 1 if up else 0)
        target[pl.ds(start + 20, 4)] = jnp.zeros((4, LANES), F32)

    for target, start, flag in (
        ((up_msg, base, next_upper), (pair_msg, 0, is_upper))
        if level == 0
        else ((up_msg, base, next_upper),)
    ):

        @pl.when(jnp.logical_not(flag))
        def _(target=target, start=start):
            faces(target, start, z_plus)

        @pl.when(flag)
        def _(target=target, start=start):
            faces(target, start, z_minus)


def spread_kernel(moved, even_got, odd_got, after, out_hbm, tops, patched, sems, *, tiles):
    del after
    lat, lats = lax.axis_index("lat"), lax.axis_size("lat")
    odd_lat = lax.rem(lat, 2) == 1
    body = pl.ds(8, 8 * tiles)
    copies = []
    for q in range(DIRS):
        if lattice_dirs[q][0] == 0:
            copies.append(pltpu.make_async_copy(moved.at[q, body], out_hbm.at[q], sems.at[q]))
            copies[-1].start()
    order = {q: j for j, q in enumerate(x_plus + x_minus)}

    def fill(dirs, got, keep):
        for j, q in enumerate(dirs):
            for k in range(tiles + 2):
                patched[order[q], pl.ds(8 * k, 8)] = moved[q, pl.ds(8 * k, 8)]
            even_z = got[pl.ds(2 * tiles * j, tiles)]
            odd_z = got[pl.ds(2 * tiles * j + tiles, tiles)]
            patched[order[q], pl.ds(out_odd(q), tiles, stride=8)] = jnp.where(keep, even_z, 0.0)
            patched[order[q], pl.ds(out_even(q), tiles, stride=8)] = jnp.where(keep, odd_z, 0.0)

    @pl.when(odd_lat)
    def _():
        fill(x_plus, even_got, lat > 0)
        fill(x_minus, odd_got, lat < lats - 1)

    @pl.when(jnp.logical_not(odd_lat))
    def _():
        fill(x_plus, odd_got, lat > 0)
        fill(x_minus, even_got, lat < lats - 1)

    for q in x_plus + x_minus:
        copies.append(
            pltpu.make_async_copy(patched.at[order[q], body], out_hbm.at[q], sems.at[q])
        )
        copies[-1].start()
    for j, q in enumerate(z_plus + z_minus):
        rows = pl.ds(8, 8) if lattice_dirs[q][2] > 0 else pl.ds(8 * tiles, 8)
        tops[pl.ds(8 * j, 8)] = patched[order[q], rows] if q in order else moved[q, rows]
    for copy in copies:
        copy.wait()


def finish_kernel(*refs, rows, tiles, levels):
    it = iter(refs)
    owns = [next(it) for _ in range(levels)]
    gots = [next(it) for _ in range(levels)]
    pair_got, offset, edge, link, tops, pops_in = [next(it) for _ in range(6)]
    pops_out, conc_out, solved, tiles_out, sems = [next(it) for _ in range(5)]
    del pops_in
    wall = lax.axis_index("wall")
    copies = []
    for j in range(len(z_plus) + len(z_minus)):
        tiles_out[pl.ds(8 * j, 8)] = tops[pl.ds(8 * j, 8)]

    def put(got, base, lower):
        for j in range(5):
            row = 8 * j if lower else 8 * (5 + j) + 4
            tiles_out[pl.ds(row, 4)] = got[pl.ds(base + 4 * j, 4)]

    pl.when(bit(wall, 0) == 1)(lambda: put(pair_got, 0, True))
    pl.when(bit(wall, 0) == 0)(lambda: put(pair_got, 0, False))
    for r in range(1, levels):
        base = 32 if r == levels - 1 else 96
        rest = lax.rem(wall, 2 ** (r + 1))
        pl.when(rest == 2**r)(functools.partial(put, gots[r], base, True))
        pl.when(rest == 2**r - 1)(functools.partial(put, gots[r], base, False))
    for j, q in enumerate(z_plus + z_minus):
        at = pl.ds(0, 8) if lattice_dirs[q][2] > 0 else pl.ds(8 * tiles - 8, 8)
        copies.append(
            pltpu.make_async_copy(tiles_out.at[pl.ds(8 * j, 8)], pops_out.at[q, at], sems.at[j])
        )
        copies[-1].start()
    half = rows // 2
    inner = []
    for h in range(2):
        top = levels - 1
        go, xo = read_ends(owns[top], h, 2)
        gr, xr = read_ends(gots[top], h, 2)
        w = (gr + xr * go) * reciprocal(1.0 - xo * xr)
        is_upper = bit(wall, top) == 1
        w_low, w_high = jnp.where(is_upper, w, 0.0), jnp.where(is_upper, 0.0, w)
        for r in range(top - 1, -1, -1):
            is_upper = bit(wall, r) == 1
            a, b = ordered(read_ends(owns[r], h), read_ends(gots[r], h), is_upper)
            top_a, low_b, _ = merge(a, b)
            new_low = top_a[0] + top_a[1] * w_low + top_a[2] * w_high
            new_high = low_b[0] + low_b[1] * w_low + low_b[2] * w_high
            w_low, w_high = (
                jnp.where(is_upper, new_low, w_low),
                jnp.where(is_upper, w_high, new_high),
            )
        at0, at1 = pl.ds(16 * (half - 1) + 8 * h, 8), pl.ds(16 * half + 8 * h, 8)
        a0 = offset[at0] + edge[at0] * w_low
        a1 = offset[at1] + edge[at1] * w_high
        k0, k1 = link[at0], link[at1]
        r = reciprocal(1.0 - k0 * k1)
        u0, u1 = (a0 + k0 * a1) * r, (a1 + k1 * a0) * r
        solved[at0] = u0
        solved[at1] = u1
        inner.append([u0, u1, w_low, w_high])
    parts = 2
    step = half // parts
    for part in range(parts):
        for i in range(part * step, (part + 1) * step):
            if i == 0:
                continue
            for h in range(2):
                u0, u1, w_low, w_high = inner[h]
                at0 = pl.ds(16 * (half - 1 - i) + 8 * h, 8)
                at1 = pl.ds(16 * (half + i) + 8 * h, 8)
                u0 = (offset[at0] + edge[at0] * w_low) + link[at0] * u0
                u1 = (offset[at1] + edge[at1] * w_high) + link[at1] * u1
                solved[at0] = u0
                solved[at1] = u1
                inner[h] = [u0, u1, w_low, w_high]
        for side in range(2):
            begin = half - (part + 1) * step if side == 0 else half + part * step
            span = pl.ds(16 * begin, 16 * step)
            copies.append(
                pltpu.make_async_copy(
                    solved.at[span], conc_out.at[span], sems.at[10 + 2 * part + side]
                )
            )
            copies[-1].start()
    for copy in copies:
        copy.wait()


def swaps(lats, walls):
    def pairs(partner):
        table = []
        for lat in range(lats):
            for wall in range(walls):
                to_lat, to_wall = partner(lat, wall)
                table.append((lat * walls + wall, to_lat * walls + to_wall))
        return table

    def odd_partner(lat, wall):
        if lat == 0 or lat == lats - 1:
            return lat, wall ^ 1
        return ((lat + 1) ^ 1) - 1, wall

    even = pairs(lambda lat, wall: (lat ^ 1, wall))
    odd = pairs(odd_partner)
    levels = []
    while 2 ** len(levels) < walls:
        flip = 2 ** (len(levels) + 1) - 1
        levels.append(pairs(lambda lat, wall: (lat, wall ^ flip)))
    return even, odd, levels


def per_device(
    populations, concentration, cell_flags, valence, diffusivity, applied_field, *, lats, walls
):
    rows, cells = populations.shape[1], populations.shape[1] * populations.shape[2]
    tiles = cells // 8
    chunks = 4
    assert populations.shape[2] == X_CELLS and lats % 2 == 0 and walls >= 4
    even, odd, levels = swaps(lats, walls)
    assert 2 ** len(levels) == walls

    def move(x, table):
        return lax.ppermute(x, ("lat", "wall"), table)

    msg_rows = 2 * tiles * 5
    moved, even_msg, odd_msg, vel_z, conc, flags = pl.pallas_call(
        functools.partial(collide_kernel, tiles=tiles, chunks=chunks),
        out_shape=(
            on_chip(DIRS, cells + 16, LANES),
            on_chip(msg_rows, LANES),
            on_chip(msg_rows, LANES),
            on_chip(cells, LANES),
            on_chip(cells * SPECIES, LANES),
            on_chip(cells, LANES, dtype=jnp.int32),
        ),
        in_specs=[ANY_SPEC] * 3 + [SMEM_SPEC] * 2,
        out_specs=(VMEM_SPEC,) * 6,
        scratch_shapes=[
            pltpu.VMEM((DIRS, cells, LANES), F32),
            pltpu.SemaphoreType.DMA((1 + 2 * chunks,)),
        ],
        compiler_params=params(),
        cost_estimate=cost(5_000_000, 3_000_000),
        name="collide",
    )(
        populations.reshape(DIRS, cells, LANES),
        concentration.reshape(cells * SPECIES, LANES),
        cell_flags.reshape(cells, LANES),
        valence,
        applied_field,
    )
    even_got, odd_got = move(even_msg, even), move(odd_msg, odd)

    offset, edge, link, ends = pl.pallas_call(
        functools.partial(eliminate_kernel, rows=rows),
        out_shape=(on_chip(cells * SPECIES, LANES),) * 3 + (on_chip(96, LANES),),
        in_specs=[VMEM_SPEC] * 3 + [SMEM_SPEC] * 3,
        out_specs=(VMEM_SPEC,) * 4,
        compiler_params=params(),
        cost_estimate=cost(5_000_000, 3_000_000),
        name="eliminate",
    )(*pin(vel_z, conc, flags), valence, diffusivity, applied_field)

    owns, gots = [ends], [move(ends, levels[0])]
    pair_got = None
    for level in range(len(levels) - 1):
        last = level == len(levels) - 2
        shapes = (on_chip((32 if last else 96) + FACE_ROWS, LANES),)
        if level == 0:
            shapes += (on_chip(FACE_ROWS, LANES),)
        sent = pl.pallas_call(
            functools.partial(relay_kernel, tiles=tiles, level=level, last=last),
            out_shape=shapes,
            in_specs=[VMEM_SPEC] * 5,
            out_specs=(VMEM_SPEC,) * len(shapes),
            compiler_params=params(),
            cost_estimate=cost(100_000, 200_000),
            name=f"relay{level}",
        )(*pin(owns[-1], gots[-1], moved, even_got, odd_got))
        owns.append(sent[0])
        gots.append(move(sent[0], levels[level + 1]))
        if level == 0:
            pair_got = move(sent[1], levels[0])

    pops_out, tops = pl.pallas_call(
        functools.partial(spread_kernel, tiles=tiles),
        out_shape=(
            jax.ShapeDtypeStruct((DIRS, cells, LANES), F32),
            on_chip(80, LANES),
        ),
        in_specs=[VMEM_SPEC] * 4,
        out_specs=(ANY_SPEC, VMEM_SPEC),
        scratch_shapes=[
            pltpu.VMEM((10, cells + 16, LANES), F32),
            pltpu.SemaphoreType.DMA((DIRS,)),
        ],
        compiler_params=params(),
        cost_estimate=cost(1_000_000, 2_500_000),
        name="spread",
    )(*pin(moved, even_got, odd_got, owns[-1]))

    n_in = 2 * len(levels) + 5
    new_pops, new_conc = pl.pallas_call(
        functools.partial(finish_kernel, rows=rows, tiles=tiles, levels=len(levels)),
        out_shape=(
            jax.ShapeDtypeStruct((DIRS, cells, LANES), F32),
            jax.ShapeDtypeStruct((cells * SPECIES, LANES), F32),
        ),
        in_specs=[VMEM_SPEC] * n_in + [ANY_SPEC],
        out_specs=(ANY_SPEC, ANY_SPEC),
        input_output_aliases={n_in: 0},
        scratch_shapes=[
            pltpu.VMEM((cells * SPECIES, LANES), F32),
            pltpu.VMEM((80, LANES), F32),
            pltpu.SemaphoreType.DMA((14,)),
        ],
        compiler_params=params(),
        cost_estimate=cost(1_000_000, 2_000_000),
        name="finish",
    )(*pin(*owns, *gots, pair_got, offset, edge, link, tops), pops_out)
    return new_pops.reshape(populations.shape), new_conc.reshape(concentration.shape)


def solution(mesh):
    in_specs = (
        P(None, "wall", "lat", None),
        P("wall", None, "lat", None),
        P("wall", "lat", None),
        P(),
        P(),
        P(),
    )
    out_specs = (P(None, "wall", "lat", None), P("wall", None, "lat", None))
    return jax.shard_map(
        functools.partial(per_device, lats=mesh.shape["lat"], walls=mesh.shape["wall"]),
        mesh=mesh,
        in_specs=in_specs,
        out_specs=out_specs,
        check_vma=False,
    )
```

profile of v0, /device:TPU:9, one launch (start us, length us, event | category | flops | bytes accessed | tf_op | source)
XLA Modules:
  0.0 18.8 jit_solution(7457375792822975699)
XLA Ops:
  0.6 0.0 copy-start.5
  0.6 0.0 copy-start
  0.7 1.3 %copy-done = f32[19,32,4,128]{3,2,1,0:T(4,128)S(1)} copy-done((f32[19,32,4,128]{3,2,1,0:T(4,128)S(1)}, f32[19,32,4,128]{3,2,1,0:T(4,128)}, u32[]{:S(2)}) %copy-start) | copy-done | bytes 1245208
  1.9 0.0 copy-start.1
  1.9 0.9 %copy-done.1 = f32[32,4,4,128]{3,2,1,0:T(4,128)S(1)} copy-done((f32[32,4,4,128]{3,2,1,0:T(4,128)S(1)}, f32[32,4,4,128]{3,2,1,0:T(4,128)}, u32[]{:S(2)}) %copy-start.1) | copy-done | bytes 262168
  2.9 0.0 copy-start.2
  2.9 0.8 %copy-done.2 = s32[32,4,128]{2,1,0:T(4,128)S(1)} copy-done((s32[32,4,128]{2,1,0:T(4,128)S(1)}, s32[32,4,128]{2,1,0:T(4,128)}, u32[]{:S(2)}) %copy-start.2) | copy-done | bytes 65560
  3.7 0.0 copy-start.3
  3.7 0.7 %copy-done.3 = s32[4]{0:T(128)S(1)} copy-done((s32[4]{0:T(128)S(1)}, s32[4]{0:T(128)}, u32[]{:S(2)}) %copy-start.3) | copy-done | bytes 40
  4.4 0.0 copy-start.4
  4.4 0.7 %copy-done.4 = f32[3]{0:T(128)S(1)} copy-done((f32[3]{0:T(128)S(1)}, f32[3]{0:T(128)}, u32[]{:S(2)}) %copy-start.4) | copy-done | bytes 36
  5.0 2.0 %collide.1 = (f32[19,144,128]{2,1,0:T(8,128)S(1)}, f32[160,128]{1,0:T(8,128)S(1)}, f32[160,128]{1,0:T(8,128)S(1)}, f32[128,128]{1,0:T(8,128)S(1)}, f32[512,128]{1,0:T(8,128)S(1)}, /*index=5*/s32[128,128]{1,0:T(8,128)S(1)}) custom-call(f32[19,128,128]{2,1,0:T(8,128)S(1)} %bitcast.5, f32[512,128]{1,0:T(8,128)S(1)} %bitcast.6, s32[128,128]{1,0:T(8,128)S(1)} %bitcast.7, ...), custom_call_target="tpu_custom_call" | custom-call | flops 5000000 | bytes 3000000 | tf_op jit(solution)/shard_map/collide/pallas_call | solution.py:544
  7.1 1.3 %collective-permute-start.1 = (f32[160,128]{1,0:T(8,128)S(1)}, f32[160,128]{1,0:T(8,128)S(1)}, u32[]{:S(2)}, u32[]{:S(2)}) collective-permute-start(f32[160,128]{1,0:T(8,128)S(1)} %get-tuple-element.23), channel_id=1, source_target_pairs={{0,4},{1,5},{2,6},{3,7},{4,0},{5,1},{6,2},{7,3},{8,12},{9,13},{10,... | collective-permute-start | bytes 245768 | tf_op jit(solution)/shard_map/ppermute | solution.py:541
  8.4 0.0 collective-permute-start.2
  8.4 0.0 copy-done.5
  8.4 0.9 %eliminate.1 = (f32[512,128]{1,0:T(8,128)S(1)}, f32[512,128]{1,0:T(8,128)S(1)}, f32[512,128]{1,0:T(8,128)S(1)}, f32[96,128]{1,0:T(8,128)S(1)}) custom-call(f32[128,128]{1,0:T(8,128)S(1)} %get-tuple-element.18.vel_z, f32[512,128]{1,0:T(8,128)S(1)} %get-tuple-element.19.conc, s32[128,128]{1,0:T(8,128)S(1)} %get-tuple-element.20.flags, s32[4]{0:T(128)S(1)} %copy-done.3, ...), custom_call_target="tpu_custom_call" | custom-call | flops 5000000 | bytes 3000000 | tf_op jit(solution)/shard_map/eliminate/pallas_call | solution.py:572
  9.3 1.0 %collective-permute-start = (f32[96,128]{1,0:T(8,128)S(1)}, f32[96,128]{1,0:T(8,128)S(1)}, u32[]{:S(2)}, u32[]{:S(2)}) collective-permute-start(f32[96,128]{1,0:T(8,128)S(1)} %get-tuple-element.21.refs_0_), channel_id=1, source_target_pairs={{0,1},{1,0},{2,3},{3,2},{4,5},{5,4},{6,7},{7,6},{8,9},{9,8},{10,11... | collective-permute-start | bytes 147464 | tf_op jit(solution)/shard_map/ppermute | solution.py:541
  10.3 0.9 %collective-permute-done.refs_1_.refs_2_ = f32[96,128]{1,0:T(8,128)S(1)} collective-permute-done((f32[96,128]{1,0:T(8,128)S(1)}, f32[96,128]{1,0:T(8,128)S(1)}, u32[]{:S(2)}, u32[]{:S(2)}) %collective-permute-start) | collective-permute-done | bytes 49184 | tf_op jit(solution)/shard_map/ppermute | solution.py:541
  11.2 0.0 collective-permute-done.1.refs_3_.even_got
  11.2 1.4 %collective-permute-done.2.refs_4_.odd_got = f32[160,128]{1,0:T(8,128)S(1)} collective-permute-done((f32[160,128]{1,0:T(8,128)S(1)}, f32[160,128]{1,0:T(8,128)S(1)}, u32[]{:S(2)}, u32[]{:S(2)}) %collective-permute-start.2) | collective-permute-done | bytes 81952 | tf_op jit(solution)/shard_map/ppermute | solution.py:541
  12.6 3.3 %collective-permute-start.3 = (f32[56,128]{1,0:T(8,128)S(1)}, f32[56,128]{1,0:T(8,128)S(1)}, u32[]{:S(2)}, u32[]{:S(2)}) collective-permute-start(f32[56,128]{1,0:T(8,128)S(1)} %get-tuple-element.25.after.refs_1_), channel_id=1, source_target_pairs={{0,3},{1,2},{2,1},{3,0},{4,7},{5,6},{6,5},{7,4},{8,11},{9,10},{10,... | collective-permute-start | bytes 86024 | tf_op jit(solution)/shard_map/ppermute | solution.py:541
  15.9 0.0 collective-permute-start.4
  15.9 1.2 %spread.1 = (f32[19,128,128]{2,1,0:T(8,128)}, f32[80,128]{1,0:T(8,128)S(1)}) custom-call(f32[19,144,128]{2,1,0:T(8,128)S(1)} %get-tuple-element.22.refs_2_.moved, f32[160,128]{1,0:T(8,128)S(1)} %collective-permute-done.1.refs_3_.even_got, f32[160,128]{1,0:T(8,128)S(1)} %collective-permute-done.2.refs_4_.odd_got, f32[56,128]{1,0:T(8,128)S(1)} %get-tuple-element.25.after.refs_1_), custom_call_target="tpu_custom_call" | custom-call | flops 1000000 | bytes 2500000 | tf_op jit(solution)/shard_map/spread/pallas_call | solution.py:603
  17.1 0.0 collective-permute-done.4.refs_4_
  17.1 0.9 %collective-permute-done.3.refs_3_ = f32[56,128]{1,0:T(8,128)S(1)} collective-permute-done((f32[56,128]{1,0:T(8,128)S(1)}, f32[56,128]{1,0:T(8,128)S(1)}, u32[]{:S(2)}, u32[]{:S(2)}) %collective-permute-start.3) | collective-permute-done | bytes 28704 | tf_op jit(solution)/shard_map/ppermute | solution.py:541
  18.0 0.9 %finish.1 = (f32[19,128,128]{2,1,0:T(8,128)}, f32[512,128]{1,0:T(8,128)}) custom-call(f32[96,128]{1,0:T(8,128)S(1)} %get-tuple-element.21.refs_0_, f32[56,128]{1,0:T(8,128)S(1)} %get-tuple-element.25.after.refs_1_, f32[96,128]{1,0:T(8,128)S(1)} %collective-permute-done.refs_1_.refs_2_, ...), custom_call_target="tpu_custom_call", output_to_operand_aliasing={{0}: (9, {})} | custom-call | flops 1000000 | bytes 2000000 | tf_op jit(solution)/shard_map/finish/pallas_call | solution.py:621
  (1 shorter events, 0.0 us)
Async XLA Ops:
  0.6 7.8 %copy-start.5 = (f32[4]{0:T(128)S(1)}, f32[4]{0:T(128)}, u32[]{:S(2)}) copy-start(f32[4]{0:T(128)} %diffusivity.1) | copy-start | bytes 52
  0.6 1.3 %copy-start = (f32[19,32,4,128]{3,2,1,0:T(4,128)S(1)}, f32[19,32,4,128]{3,2,1,0:T(4,128)}, u32[]{:S(2)}) copy-start(f32[19,32,4,128]{3,2,1,0:T(4,128)} %param.6) | copy-start | bytes 3735556
  1.9 0.9 %copy-start.1 = (f32[32,4,4,128]{3,2,1,0:T(4,128)S(1)}, f32[32,4,4,128]{3,2,1,0:T(4,128)}, u32[]{:S(2)}) copy-start(f32[32,4,4,128]{3,2,1,0:T(4,128)} %param.7) | copy-start | bytes 786436
  2.9 0.8 %copy-start.2 = (s32[32,4,128]{2,1,0:T(4,128)S(1)}, s32[32,4,128]{2,1,0:T(4,128)}, u32[]{:S(2)}) copy-start(s32[32,4,128]{2,1,0:T(4,128)} %param.8) | copy-start | bytes 196612
  3.7 0.7 %copy-start.3 = (s32[4]{0:T(128)S(1)}, s32[4]{0:T(128)}, u32[]{:S(2)}) copy-start(s32[4]{0:T(128)} %valence.3) | copy-start | bytes 52
  4.4 0.7 %copy-start.4 = (f32[3]{0:T(128)S(1)}, f32[3]{0:T(128)}, u32[]{:S(2)}) copy-start(f32[3]{0:T(128)} %field.3) | copy-start | bytes 40
  7.1 4.1 %collective-permute-start.1 = (f32[160,128]{1,0:T(8,128)S(1)}, f32[160,128]{1,0:T(8,128)S(1)}, u32[]{:S(2)}, u32[]{:S(2)}) collective-permute-start(f32[160,128]{1,0:T(8,128)S(1)} %get-tuple-element.23), channel_id=1, source_target_pairs={{0,4},{1,5},{2,6},{3,7},{4,0},{5,1},{6,2},{7,3},{8,12},{9,13},{10,... | collective-permute-start | bytes 245768 | tf_op jit(solution)/shard_map/ppermute | solution.py:541
  8.4 4.2 %collective-permute-start.2 = (f32[160,128]{1,0:T(8,128)S(1)}, f32[160,128]{1,0:T(8,128)S(1)}, u32[]{:S(2)}, u32[]{:S(2)}) collective-permute-start(f32[160,128]{1,0:T(8,128)S(1)} %get-tuple-element.24), channel_id=1, source_target_pairs={{0,1},{1,0},{2,3},{3,2},{4,8},{5,9},{6,10},{7,11},{8,4},{9,5},{10,... | collective-permute-start | bytes 245768 | tf_op jit(solution)/shard_map/ppermute | solution.py:541
  9.3 1.9 %collective-permute-start = (f32[96,128]{1,0:T(8,128)S(1)}, f32[96,128]{1,0:T(8,128)S(1)}, u32[]{:S(2)}, u32[]{:S(2)}) collective-permute-start(f32[96,128]{1,0:T(8,128)S(1)} %get-tuple-element.21.refs_0_), channel_id=1, source_target_pairs={{0,1},{1,0},{2,3},{3,2},{4,5},{5,4},{6,7},{7,6},{8,9},{9,8},{10,11... | collective-permute-start | bytes 147464 | tf_op jit(solution)/shard_map/ppermute | solution.py:541
  12.6 5.3 %collective-permute-start.3 = (f32[56,128]{1,0:T(8,128)S(1)}, f32[56,128]{1,0:T(8,128)S(1)}, u32[]{:S(2)}, u32[]{:S(2)}) collective-permute-start(f32[56,128]{1,0:T(8,128)S(1)} %get-tuple-element.25.after.refs_1_), channel_id=1, source_target_pairs={{0,3},{1,2},{2,1},{3,0},{4,7},{5,6},{6,5},{7,4},{8,11},{9,10},{10,... | collective-permute-start | bytes 86024 | tf_op jit(solution)/shard_map/ppermute | solution.py:541
  15.9 1.2 %collective-permute-start.4 = (f32[24,128]{1,0:T(8,128)S(1)}, f32[24,128]{1,0:T(8,128)S(1)}, u32[]{:S(2)}, u32[]{:S(2)}) collective-permute-start(f32[24,128]{1,0:T(8,128)S(1)} %get-tuple-element.26), channel_id=1, source_target_pairs={{0,1},{1,0},{2,3},{3,2},{4,5},{5,4},{6,7},{7,6},{8,9},{9,8},{10,11... | collective-permute-start | bytes 36872 | tf_op jit(solution)/shard_map/ppermute | solution.py:541
where the time goes:
time: 19.1 us; the launch traced here: 18.8 us
  starting transfers between devices  5.62 us (29%)
  Pallas kernels  4.99 us (26%)
  local copies, waits for them, and re-layouts  4.39 us (23%)
  waiting for transfers between devices  3.14 us (16%)
  between operations  0.7 us (4%)
    ppermute x5, starting transfers between devices, move(): return lax.ppermute(x, ('lat', 'wall'), table)  5.62 us
    unnamed x12, local copies, waits for them, and re-layouts  4.39 us
    ppermute x5, waiting for transfers between devices, move(): return lax.ppermute(x, ('lat', 'wall'), table)  3.14 us
    pallas_call x1, Pallas kernels, per_device(): pl.pallas_call(functools.partial(collide_kernel, tiles=tiles, chunks=chun...  2.01 us
    pallas_call x1, Pallas kernels, per_device(): pl.pallas_call(functools.partial(spread_kernel, tiles=tiles), out_shape=(...  1.18 us
    pallas_call x1, Pallas kernels, per_device(): pl.pallas_call(functools.partial(finish_kernel, rows=rows, tiles=tiles, l...  0.88 us
    pallas_call x1, Pallas kernels, per_device(): pl.pallas_call(functools.partial(eliminate_kernel, rows=rows), out_shape=...  0.88 us
  transfers between devices with their start and end apart: 5, of which 3 were waited for; matrix products, arithmetic and copies ran while one was open for 0% of the time, Pallas kernels for 11%

commit v1 on v0

--- a/solution.py
+++ b/solution.py
@@ -42,7 +42,6 @@
 FACE_ROWS = 24
 
 VMEM_SPEC = pl.BlockSpec(memory_space=pltpu.VMEM)
-SMEM_SPEC = pl.BlockSpec(memory_space=pltpu.SMEM)
 ANY_SPEC = pl.BlockSpec(memory_space=pl.ANY)
 
 
@@ -56,6 +55,10 @@
 
 def cost(flops, nbytes):
     return pl.CostEstimate(flops=flops, bytes_accessed=nbytes, transcendentals=0)
+
+
+def in_hbm(*arrays):
+    return [pltpu.with_memory_space_constraint(a, pltpu.HBM) for a in arrays]
 
 
 def pin(*arrays):
@@ -80,35 +83,53 @@
     pops_hbm,
     conc_hbm,
     flags_hbm,
-    valence,
-    field,
+    valence_hbm,
+    diffusivity_hbm,
+    field_hbm,
     moved,
     even_msg,
     odd_msg,
     vel_z,
     conc,
     flags,
+    table,
     pops,
+    valence,
+    diffusivity,
+    field,
     sems,
     *,
-    tiles,
     chunks,
 ):
-    per = tiles // chunks * 8
-    copies = []
-    flag_copy = pltpu.make_async_copy(flags_hbm, flags, sems.at[0])
-    flag_copy.start()
-    for c in range(chunks):
-        rows = pl.ds(c * per, per)
-        crows = pl.ds(c * per * SPECIES, per * SPECIES)
-        pair = (
-            pltpu.make_async_copy(conc_hbm.at[crows], conc.at[crows], sems.at[1 + 2 * c]),
-            pltpu.make_async_copy(pops_hbm.at[:, rows], pops.at[:, rows], sems.at[2 + 2 * c]),
-        )
-        for copy in pair:
+    tiles = sum(chunks)
+    small = [
+        pltpu.make_async_copy(source, target, sems.at[i])
+        for i, (source, target) in enumerate(
+            (
+                (flags_hbm, flags),
+                (valence_hbm, valence),
+                (field_hbm, field),
+                (diffusivity_hbm, diffusivity),
+            )
+        )
+    ]
+    for copy in small:
+        copy.start()
+    copies = {}
+    at = 0
+    for c, count in enumerate(chunks):
+        rows = pl.ds(8 * at, 8 * count)
+        crows = pl.ds(8 * SPECIES * at, 8 * SPECIES * count)
+        copies[at] = (
+            pltpu.make_async_copy(conc_hbm.at[crows], conc.at[crows], sems.at[4 + 2 * c]),
+            pltpu.make_async_copy(pops_hbm.at[:, rows], pops.at[:, rows], sems.at[5 + 2 * c]),
+        )
+        for copy in copies[at]:
             copy.start()
-        copies.append(pair)
+        at += count
     low = low_rows()
+    for copy in small:
+        copy.wait()
     val_pair = [
         jnp.where(low, valence[2 * h].astype(F32), valence[2 * h + 1].astype(F32))
         for h in range(2)
@@ -116,11 +137,9 @@
     field_xyz = [FORCE_GAIN * field[axis] for axis in range(3)]
     zero = jnp.zeros((8, LANES), F32)
     held = {q: zero for q in z_plus + z_minus}
-    flag_copy.wait()
     for k in range(tiles):
-        if k % (tiles // chunks) == 0:
-            for copy in copies[k // (tiles // chunks)]:
-                copy.wait()
+        for copy in copies.get(k, ()):
+            copy.wait()
         p = [pops[q, pl.ds(8 * k, 8)] for q in range(DIRS)]
         solid = flags[pl.ds(8 * k, 8)] != 0
         sums = []
@@ -215,22 +234,29 @@
         pack(even_msg, x_minus)
         pack(odd_msg, x_plus)
 
+    for h in range(2):
+        diff = jnp.where(low, diffusivity[2 * h], diffusivity[2 * h + 1])
+        values = (
+            diff,
+            diff * 0.01,
+            diff * jnp.where(val_pair[h] > 0, 0.5, 0.02),
+            val_pair[h] * field[2],
+        )
+        for j, value in enumerate(values):
+            table[pl.ds(8 * (4 * h + j), 8)] = value
+
 
 def reciprocal(x):
     return 1.0 / x
 
 
 def eliminate_kernel(
-    vel_z, conc, flags, valence, diffusivity, field, offset, edge, link, ends, *, rows
+    vel_z, conc, flags, table, offset, edge, link, ends, *, rows
 ):
     low = low_rows()
     half = rows // 2
     for h in range(2):
-        val = jnp.where(low, valence[2 * h].astype(F32), valence[2 * h + 1].astype(F32))
-        diff = jnp.where(low, diffusivity[2 * h], diffusivity[2 * h + 1])
-        slow = diff * 0.01
-        membrane = diff * jnp.where(val > 0, 0.5, 0.02)
-        pull = val * field[2]
+        diff, slow, membrane, pull = [table[pl.ds(8 * (4 * h + j), 8)] for j in range(4)]
 
         def coefficients(z):
             tile = pl.ds(8 * (z // 2), 8)
@@ -532,7 +558,8 @@
 ):
     rows, cells = populations.shape[1], populations.shape[1] * populations.shape[2]
     tiles = cells // 8
-    chunks = 4
+    chunks = [tiles // 8, tiles // 4]
+    chunks += [(tiles - sum(chunks)) // 2, (tiles - sum(chunks) + 1) // 2]
     assert populations.shape[2] == X_CELLS and lats % 2 == 0 and walls >= 4
     even, odd, levels = swaps(lats, walls)
     assert 2 ** len(levels) == walls
@@ -541,8 +568,8 @@
         return lax.ppermute(x, ("lat", "wall"), table)
 
     msg_rows = 2 * tiles * 5
-    moved, even_msg, odd_msg, vel_z, conc, flags = pl.pallas_call(
-        functools.partial(collide_kernel, tiles=tiles, chunks=chunks),
+    moved, even_msg, odd_msg, vel_z, conc, flags, table = pl.pallas_call(
+        functools.partial(collide_kernel, chunks=chunks),
         out_shape=(
             on_chip(DIRS, cells + 16, LANES),
             on_chip(msg_rows, LANES),
@@ -550,34 +577,41 @@
             on_chip(cells, LANES),
             on_chip(cells * SPECIES, LANES),
             on_chip(cells, LANES, dtype=jnp.int32),
+            on_chip(64, LANES),
         ),
-        in_specs=[ANY_SPEC] * 3 + [SMEM_SPEC] * 2,
-        out_specs=(VMEM_SPEC,) * 6,
+        in_specs=[ANY_SPEC] * 6,
+        out_specs=(VMEM_SPEC,) * 7,
         scratch_shapes=[
             pltpu.VMEM((DIRS, cells, LANES), F32),
-            pltpu.SemaphoreType.DMA((1 + 2 * chunks,)),
+            pltpu.SMEM((SPECIES,), jnp.int32),
+            pltpu.SMEM((SPECIES,), F32),
+            pltpu.SMEM((3,), F32),
+            pltpu.SemaphoreType.DMA((4 + 2 * len(chunks),)),
         ],
         compiler_params=params(),
         cost_estimate=cost(5_000_000, 3_000_000),
         name="collide",
     )(
-        populations.reshape(DIRS, cells, LANES),
-        concentration.reshape(cells * SPECIES, LANES),
-        cell_flags.reshape(cells, LANES),
-        valence,
-        applied_field,
+        *in_hbm(
+            populations.reshape(DIRS, cells, LANES),
+            concentration.reshape(cells * SPECIES, LANES),
+            cell_flags.reshape(cells, LANES),
+            valence,
+            diffusivity,
+            applied_field,
+        )
     )
     even_got, odd_got = move(even_msg, even), move(odd_msg, odd)
 
     offset, edge, link, ends = pl.pallas_call(
         functools.partial(eliminate_kernel, rows=rows),
         out_shape=(on_chip(cells * SPECIES, LANES),) * 3 + (on_chip(96, LANES),),
-        in_specs=[VMEM_SPEC] * 3 + [SMEM_SPEC] * 3,
+        in_specs=[VMEM_SPEC] * 4,
         out_specs=(VMEM_SPEC,) * 4,
         compiler_params=params(),
         cost_estimate=cost(5_000_000, 3_000_000),
         name="eliminate",
-    )(*pin(vel_z, conc, flags), valence, diffusivity, applied_field)
+    )(*pin(vel_z, conc, flags, table))
 
     owns, gots = [ends], [move(ends, levels[0])]
     pair_got = None

time: 19.1 us -> 14.5 us (0.76)
  local copies, waits for them, and re-layouts: 4.39 us -> 0 us
  Pallas kernels: 4.99 us -> 4.39 us
  waiting for transfers between devices: 3.14 us -> 3.7 us
    unnamed x12 -> x0, local copies, waits for them, and re-layouts: 4.39 us -> none
    ppermute x5, waiting for transfers between devices: 3.14 us -> 3.7 us  [move(): return lax.ppermute(x, ('lat', 'wall'), table)]
    pallas_call x1, Pallas kernels: 0.88 us -> 0.32 us  [per_device(): pl.pallas_call(functools.partial(eliminate_kernel, rows=rows), out_shape=...]
  transfers between devices with their start and end apart: 5 -> 5, of which waited for: 3 -> 3; matrix products, arithmetic and copies ran while one was open for 0% -> 0% of each run, Pallas kernels for 11% -> 10%
where the time goes in v1:
time: 14.5 us; the launch traced here: 14.4 us
  starting transfers between devices  5.62 us (39%)
  Pallas kernels  4.39 us (30%)
  waiting for transfers between devices  3.7 us (26%)
  between operations  0.67 us (5%)
    ppermute x5, starting transfers between devices, move(): return lax.ppermute(x, ('lat', 'wall'), table)  5.62 us
    ppermute x5, waiting for transfers between devices, move(): return lax.ppermute(x, ('lat', 'wall'), table)  3.7 us
    pallas_call x1, Pallas kernels, per_device(): pl.pallas_call(functools.partial(collide_kernel, chunks=chunks), out_shap...  1.98 us
    pallas_call x1, Pallas kernels, per_device(): pl.pallas_call(functools.partial(spread_kernel, tiles=tiles), out_shape=(...  1.18 us
    pallas_call x1, Pallas kernels, per_device(): pl.pallas_call(functools.partial(finish_kernel, rows=rows, tiles=tiles, l...  0.87 us
    pallas_call x1, Pallas kernels, per_device(): pl.pallas_call(functools.partial(eliminate_kernel, rows=rows), out_shape=...  0.32 us
  transfers between devices with their start and end apart: 5, of which 3 were waited for; matrix products, arithmetic and copies ran while one was open for 0% of the time, Pallas kernels for 10%

profile of v1, /device:TPU:9, one launch (start us, length us, event | category | flops | bytes accessed | tf_op | source)
XLA Modules:
  0.0 14.4 jit_solution(4580475844960368974)
XLA Ops:
  0.6 2.0 %collide.1 = (f32[19,144,128]{2,1,0:T(8,128)S(1)}, f32[160,128]{1,0:T(8,128)S(1)}, f32[160,128]{1,0:T(8,128)S(1)}, f32[128,128]{1,0:T(8,128)S(1)}, f32[512,128]{...) custom-call(f32[19,128,128]{2,1,0:T(8,128)} %bitcast.5, f32[512,128]{1,0:T(8,128)} %bitcast.7, ...), custom_call_target="tpu_custom_call" | custom-call | flops 5000000 | bytes 3000000 | tf_op jit(solution)/shard_map/collide/pallas_call | solution.py:571
  2.6 1.3 %collective-permute-start.1 = (f32[160,128]{1,0:T(8,128)S(1)}, f32[160,128]{1,0:T(8,128)S(1)}, u32[]{:S(2)}, u32[]{:S(2)}) collective-permute-start(f32[160,128]{1,0:T(8,128)S(1)} %get-tuple-element.25), channel_id=1, source_target_pairs={{0,4},{1,5},{2,6},{3,7},{4,0},{5,1},{6,2},{7,3},{8,12},{9,13},{10,... | collective-permute-start | bytes 245768 | tf_op jit(solution)/shard_map/ppermute | solution.py:568
  3.9 0.0 collective-permute-start.2
  4.0 0.3 %eliminate.1 = (f32[512,128]{1,0:T(8,128)S(1)}, f32[512,128]{1,0:T(8,128)S(1)}, f32[512,128]{1,0:T(8,128)S(1)}, f32[96,128]{1,0:T(8,128)S(1)}) custom-call(f32[128,128]{1,0:T(8,128)S(1)} %get-tuple-element.19.vel_z, f32[512,128]{1,0:T(8,128)S(1)} %get-tuple-element.20.conc, s32[128,128]{1,0:T(8,128)S(1)} %get-tuple-element.21.flags, ...), custom_call_target="tpu_custom_call" | custom-call | flops 5000000 | bytes 3000000 | tf_op jit(solution)/shard_map/eliminate/pallas_call | solution.py:606
  4.3 1.0 %collective-permute-start = (f32[96,128]{1,0:T(8,128)S(1)}, f32[96,128]{1,0:T(8,128)S(1)}, u32[]{:S(2)}, u32[]{:S(2)}) collective-permute-start(f32[96,128]{1,0:T(8,128)S(1)} %get-tuple-element.23.refs_0_), channel_id=1, source_target_pairs={{0,1},{1,0},{2,3},{3,2},{4,5},{5,4},{6,7},{7,6},{8,9},{9,8},{10,11... | collective-permute-start | bytes 147464 | tf_op jit(solution)/shard_map/ppermute | solution.py:568
  5.3 0.9 %collective-permute-done.refs_1_.refs_2_ = f32[96,128]{1,0:T(8,128)S(1)} collective-permute-done((f32[96,128]{1,0:T(8,128)S(1)}, f32[96,128]{1,0:T(8,128)S(1)}, u32[]{:S(2)}, u32[]{:S(2)}) %collective-permute-start) | collective-permute-done | bytes 49184 | tf_op jit(solution)/shard_map/ppermute | solution.py:568
  6.2 0.0 collective-permute-done.1.refs_3_.even_got
  6.2 2.0 %collective-permute-done.2.refs_4_.odd_got = f32[160,128]{1,0:T(8,128)S(1)} collective-permute-done((f32[160,128]{1,0:T(8,128)S(1)}, f32[160,128]{1,0:T(8,128)S(1)}, u32[]{:S(2)}, u32[]{:S(2)}) %collective-permute-start.2) | collective-permute-done | bytes 81952 | tf_op jit(solution)/shard_map/ppermute | solution.py:568
  8.2 3.3 %collective-permute-start.3 = (f32[56,128]{1,0:T(8,128)S(1)}, f32[56,128]{1,0:T(8,128)S(1)}, u32[]{:S(2)}, u32[]{:S(2)}) collective-permute-start(f32[56,128]{1,0:T(8,128)S(1)} %get-tuple-element.27.after.refs_1_), channel_id=1, source_target_pairs={{0,3},{1,2},{2,1},{3,0},{4,7},{5,6},{6,5},{7,4},{8,11},{9,10},{10,... | collective-permute-start | bytes 86024 | tf_op jit(solution)/shard_map/ppermute | solution.py:568
  11.5 0.0 collective-permute-start.4
  11.5 1.2 %spread.1 = (f32[19,128,128]{2,1,0:T(8,128)}, f32[80,128]{1,0:T(8,128)S(1)}) custom-call(f32[19,144,128]{2,1,0:T(8,128)S(1)} %get-tuple-element.24.refs_2_.moved, f32[160,128]{1,0:T(8,128)S(1)} %collective-permute-done.1.refs_3_.even_got, f32[160,128]{1,0:T(8,128)S(1)} %collective-permute-done.2.refs_4_.odd_got, f32[56,128]{1,0:T(8,128)S(1)} %get-tuple-element.27.after.refs_1_), custom_call_target="tpu_custom_call" | custom-call | flops 1000000 | bytes 2500000 | tf_op jit(solution)/shard_map/spread/pallas_call | solution.py:637
  12.6 0.0 collective-permute-done.4.refs_4_
  12.7 0.9 %collective-permute-done.3.refs_3_ = f32[56,128]{1,0:T(8,128)S(1)} collective-permute-done((f32[56,128]{1,0:T(8,128)S(1)}, f32[56,128]{1,0:T(8,128)S(1)}, u32[]{:S(2)}, u32[]{:S(2)}) %collective-permute-start.3) | collective-permute-done | bytes 28704 | tf_op jit(solution)/shard_map/ppermute | solution.py:568
  13.5 0.9 %finish.1 = (f32[19,128,128]{2,1,0:T(8,128)}, f32[512,128]{1,0:T(8,128)}) custom-call(f32[96,128]{1,0:T(8,128)S(1)} %get-tuple-element.23.refs_0_, f32[56,128]{1,0:T(8,128)S(1)} %get-tuple-element.27.after.refs_1_, f32[96,128]{1,0:T(8,128)S(1)} %collective-permute-done.refs_1_.refs_2_, ...), custom_call_target="tpu_custom_call", output_to_operand_aliasing={{0}: (9, {})} | custom-call | flops 1000000 | bytes 2000000 | tf_op jit(solution)/shard_map/finish/pallas_call | solution.py:655
  (1 shorter events, 0.0 us)
Async XLA Ops:
  2.6 3.6 %collective-permute-start.1 = (f32[160,128]{1,0:T(8,128)S(1)}, f32[160,128]{1,0:T(8,128)S(1)}, u32[]{:S(2)}, u32[]{:S(2)}) collective-permute-start(f32[160,128]{1,0:T(8,128)S(1)} %get-tuple-element.25), channel_id=1, source_target_pairs={{0,4},{1,5},{2,6},{3,7},{4,0},{5,1},{6,2},{7,3},{8,12},{9,13},{10,... | collective-permute-start | bytes 245768 | tf_op jit(solution)/shard_map/ppermute | solution.py:568
  3.9 4.2 %collective-permute-start.2 = (f32[160,128]{1,0:T(8,128)S(1)}, f32[160,128]{1,0:T(8,128)S(1)}, u32[]{:S(2)}, u32[]{:S(2)}) collective-permute-start(f32[160,128]{1,0:T(8,128)S(1)} %get-tuple-element.26), channel_id=1, source_target_pairs={{0,1},{1,0},{2,3},{3,2},{4,8},{5,9},{6,10},{7,11},{8,4},{9,5},{10,... | collective-permute-start | bytes 245768 | tf_op jit(solution)/shard_map/ppermute | solution.py:568
  4.3 1.9 %collective-permute-start = (f32[96,128]{1,0:T(8,128)S(1)}, f32[96,128]{1,0:T(8,128)S(1)}, u32[]{:S(2)}, u32[]{:S(2)}) collective-permute-start(f32[96,128]{1,0:T(8,128)S(1)} %get-tuple-element.23.refs_0_), channel_id=1, source_target_pairs={{0,1},{1,0},{2,3},{3,2},{4,5},{5,4},{6,7},{7,6},{8,9},{9,8},{10,11... | collective-permute-start | bytes 147464 | tf_op jit(solution)/shard_map/ppermute | solution.py:568
  8.2 5.3 %collective-permute-start.3 = (f32[56,128]{1,0:T(8,128)S(1)}, f32[56,128]{1,0:T(8,128)S(1)}, u32[]{:S(2)}, u32[]{:S(2)}) collective-permute-start(f32[56,128]{1,0:T(8,128)S(1)} %get-tuple-element.27.after.refs_1_), channel_id=1, source_target_pairs={{0,3},{1,2},{2,1},{3,0},{4,7},{5,6},{6,5},{7,4},{8,11},{9,10},{10,... | collective-permute-start | bytes 86024 | tf_op jit(solution)/shard_map/ppermute | solution.py:568
  11.5 1.2 %collective-permute-start.4 = (f32[24,128]{1,0:T(8,128)S(1)}, f32[24,128]{1,0:T(8,128)S(1)}, u32[]{:S(2)}, u32[]{:S(2)}) collective-permute-start(f32[24,128]{1,0:T(8,128)S(1)} %get-tuple-element.28), channel_id=1, source_target_pairs={{0,1},{1,0},{2,3},{3,2},{4,5},{5,4},{6,7},{7,6},{8,9},{9,8},{10,11... | collective-permute-start | bytes 36872 | tf_op jit(solution)/shard_map/ppermute | solution.py:568

commit v2 on v1

--- a/solution.py
+++ b/solution.py
@@ -94,6 +94,7 @@
     flags,
     table,
     pops,
+    mid,
     valence,
     diffusivity,
     field,
@@ -121,11 +122,15 @@
         rows = pl.ds(8 * at, 8 * count)
         crows = pl.ds(8 * SPECIES * at, 8 * SPECIES * count)
         copies[at] = (
-            pltpu.make_async_copy(conc_hbm.at[crows], conc.at[crows], sems.at[4 + 2 * c]),
-            pltpu.make_async_copy(pops_hbm.at[:, rows], pops.at[:, rows], sems.at[5 + 2 * c]),
+            pltpu.make_async_copy(conc_hbm.at[crows], conc.at[crows], sems.at[4 + c]),
+            pltpu.make_async_copy(
+                pops_hbm.at[:, rows], pops.at[pl.ds(0, DIRS), rows], sems.at[4 + c]
+            ),
         )
         for copy in copies[at]:
             copy.start()
+        both = pops.at[:, rows]
+        copies[at] = pltpu.make_async_copy(both, both, sems.at[4 + c])
         at += count
     low = low_rows()
     for copy in small:
@@ -135,27 +140,20 @@
         for h in range(2)
     ]
     field_xyz = [FORCE_GAIN * field[axis] for axis in range(3)]
-    zero = jnp.zeros((8, LANES), F32)
-    held = {q: zero for q in z_plus + z_minus}
-    for k in range(tiles):
-        for copy in copies.get(k, ()):
-            copy.wait()
-        p = [pops[q, pl.ds(8 * k, 8)] for q in range(DIRS)]
-        solid = flags[pl.ds(8 * k, 8)] != 0
+
+    def moments(at):
+        p = [pops[q, pl.ds(at, 8)] for q in range(DIRS)]
         sums = []
         for z in range(2):
-            part = val_pair[0] * conc[pl.ds(32 * k + 16 * z, 8)]
-            part = part + val_pair[1] * conc[pl.ds(32 * k + 16 * z + 8, 8)]
+            part = val_pair[0] * conc[pl.ds(4 * at + 16 * z, 8)]
+            part = part + val_pair[1] * conc[pl.ds(4 * at + 16 * z + 8, 8)]
             sums.append(part + pltpu.roll(part, 4, axis=0))
         charge = jnp.where(low, sums[0], sums[1])
-        force = [charge * f for f in field_xyz]
         diff = {q: p[q] - p[q + 1] for q in range(1, DIRS, 2)}
         total = {q: p[q] + p[q + 1] for q in range(1, DIRS, 2)}
         density = (
-            (p[0] + total[1])
-            + (total[3] + total[5])
-            + (total[7] + total[9])
-            + (total[11] + total[13])
+            ((p[0] + total[1]) + (total[3] + total[5]))
+            + ((total[7] + total[9]) + (total[11] + total[13]))
             + (total[15] + total[17])
         )
         momentum = [
@@ -163,57 +161,64 @@
             (diff[3] + diff[7]) - (diff[9] - diff[15]) + diff[17],
             (diff[5] + diff[11]) - (diff[13] - diff[15]) - diff[17],
         ]
+        force = [charge * f for f in field_xyz]
         inverse = 1.0 / density
         vel = [(momentum[a] + 0.5 * force[a]) * inverse for a in range(3)]
-        vel_z[pl.ds(8 * k, 8)] = vel[2]
+        vel_z[pl.ds(at, 8)] = vel[2]
         speed_sq = vel[0] * vel[0] + vel[1] * vel[1] + vel[2] * vel[2]
         work = vel[0] * force[0] + vel[1] * force[1] + vel[2] * force[2]
-        base = (1.25 * density) * (1.0 - 1.5 * speed_sq) - 1.125 * work
-        odd36 = [(3.75 / 36.0) * density * vel[a] + (1.125 / 36.0) * force[a] for a in range(3)]
-        even36 = [(5.625 / 36.0) * density * vel[a] + (3.375 / 36.0) * force[a] for a in range(3)]
-        base36 = base * (1.0 / 36.0)
-        base18 = base * (1.0 / 18.0)
-        for q in range(DIRS):
-            if q == 0:
-                results = [(0, -0.25 * p[0] + base * (1.0 / 3.0), p[0])]
-            elif q % 2 == 1:
-                axes = [(a, lattice_dirs[q][a]) for a in range(3) if lattice_dirs[q][a]]
-
-                def along(v):
-                    out = v[axes[0][0]]
-                    for a, sign in axes[1:]:
-                        out = out + v[a] if sign > 0 else out - v[a]
-                    return out
-
-                cu, odd, even = along(vel), along(odd36), along(even36)
-                if len(axes) == 1:
-                    shared = base18 + 2.0 * (cu * even)
-                    odd = 2.0 * odd
-                else:
-                    shared = base36 + cu * even
-                results = [
-                    (q, (shared + odd) - 0.25 * p[q], p[q + 1]),
-                    (q + 1, (shared - odd) - 0.25 * p[q + 1], p[q]),
-                ]
+        base = (1.25 / 36.0 * density) * (1.0 - 1.5 * speed_sq) - (1.125 / 36.0) * work
+        odd = [(3.75 / 36.0) * momentum[a] + (3.0 / 36.0) * force[a] for a in range(3)]
+        even = [(5.625 / 36.0) * momentum[a] + (6.1875 / 36.0) * force[a] for a in range(3)]
+        for j, value in enumerate((base, *vel, *odd, *even)):
+            mid[j, pl.ds(at, 8)] = value
+
+    def scatter(at):
+        solid = flags[pl.ds(at, 8)] != 0
+        base36, *rest = [mid[j, pl.ds(at, 8)] for j in range(10)]
+        vel, odd36, even36 = rest[:3], rest[3:6], rest[6:]
+        base18 = base36 + base36
+        p0 = pops[0, pl.ds(at, 8)]
+        moved[0, pl.ds(8 + at, 8)] = jnp.where(solid, p0, 12.0 * base36 - 0.25 * p0)
+        for q in range(1, DIRS, 2):
+            axes = [(a, lattice_dirs[q][a]) for a in range(3) if lattice_dirs[q][a]]
+
+            def along(v):
+                out = v[axes[0][0]]
+                for a, sign in axes[1:]:
+                    out = out + v[a] if sign > 0 else out - v[a]
+                return out
+
+            cu, odd, even = along(vel), along(odd36), along(even36)
+            if len(axes) == 1:
+                shared = base18 + 2.0 * (cu * even)
+                odd = odd + odd
             else:
-                continue
-            for d, relaxed, bounced in results:
+                shared = base36 + cu * even
+            ahead, behind = pops[q, pl.ds(at, 8)], pops[q + 1, pl.ds(at, 8)]
+            for d, relaxed, bounced in (
+                (q, (shared + odd) - 0.25 * ahead, behind),
+                (q + 1, (shared - odd) - 0.25 * behind, ahead),
+            ):
                 step_x, step_y, step_z = lattice_dirs[d]
                 value = jnp.where(solid, bounced, relaxed)
                 if step_y:
                     value = pltpu.roll(value, step_y % LANES, axis=1)
-                shift = (step_x + 4 * step_z) % 8
-                if shift:
-                    value = pltpu.roll(value, shift, axis=0)
-                if step_z == 0:
-                    moved[d, pl.ds(8 + 8 * k, 8)] = value
-                else:
-                    at = 8 + 8 * k if step_z > 0 else 8 * k
-                    moved[d, pl.ds(at, 8)] = jnp.where(low, held[d], value)
-                    held[d] = value
+                if step_x:
+                    value = pltpu.roll(value, step_x % 8, axis=0)
+                moved[d, pl.ds(8 + at + 4 * step_z, 8)] = value
+
+    at = 0
+    for count in chunks:
+        copies[at].wait()
+        for k in range(at, at + count):
+            moments(8 * k)
+        for k in range(at, at + count):
+            scatter(8 * k)
+        at += count
     for d in z_plus + z_minus:
-        at = 8 + 8 * tiles if lattice_dirs[d][2] > 0 else 8 * tiles
-        moved[d, pl.ds(at, 8)] = jnp.where(low, held[d], zero)
+        at = 8 if lattice_dirs[d][2] > 0 else 8 * tiles + 4
+        moved[d, pl.ds(at, 4)] = jnp.zeros((4, LANES), F32)
 
     def pack(target, dirs):
         for j, q in enumerate(dirs):
@@ -342,138 +347,53 @@
     return top_a, low_b, merged
 
 
-def relay_kernel(*refs, tiles, level, last):
-    own, got, moved, even_got, odd_got = refs[:5]
-    up_msg = refs[5]
-    pair_msg = refs[6] if level == 0 else None
-    wall, lat = lax.axis_index("wall"), lax.axis_index("lat")
-    lats = lax.axis_size("lat")
+def relay_kernel(own, got, send, *, level, last):
+    wall = lax.axis_index("wall")
     is_upper = bit(wall, level) == 1
     next_upper = bit(wall, level + 1) == 1
     for h in range(2):
         a, b = ordered(read_ends(own, h), read_ends(got, h), is_upper)
-        merged = merge(a, b)[2]
+        values = merge(a, b)[2]
         if last:
-            send = [
-                jnp.where(next_upper, merged[0], merged[3]),
-                jnp.where(next_upper, merged[1], merged[5]),
+            values = [
+                jnp.where(next_upper, values[0], values[3]),
+                jnp.where(next_upper, values[1], values[5]),
             ]
-        else:
-            send = merged
-        for j, value in enumerate(send):
-            up_msg[pl.ds(16 * j + 8 * h, 8)] = value
-    base = 32 if last else 96
+        for j, value in enumerate(values):
+            send[pl.ds(16 * j + 8 * h, 8)] = value
+
+
+def faces_kernel(moved, even_got, odd_got, *targets, tiles):
+    wall, lat = lax.axis_index("wall"), lax.axis_index("lat")
+    lats = lax.axis_size("lat")
     odd_lat = lax.rem(lat, 2) == 1
-    part = 2 * tiles
 
     def from_lat(q, odd_z, index):
         dirs = x_plus if q in x_plus else x_minus
-        j = dirs.index(q)
-        at = pl.ds(part * j + (tiles if odd_z else 0) + index, 1)
+        at = pl.ds(2 * tiles * dirs.index(q) + (tiles if odd_z else 0) + index, 1)
         use_even = odd_lat if q in x_plus else jnp.logical_not(odd_lat)
         exists = lat > 0 if q in x_plus else lat < lats - 1
         row = jnp.where(use_even, even_got[at], odd_got[at])
         return jnp.where(exists, row, 0.0)
 
-    def faces(target, start, dirs):
+    def fill(target, dirs):
         for j, q in enumerate(dirs):
             up = lattice_dirs[q][2] > 0
-            rows = pl.ds(8 * tiles + 8, 4) if up else pl.ds(4, 4)
-            target[pl.ds(start + 4 * j, 4)] = moved[q, rows]
+            target[pl.ds(4 * j, 4)] = moved[q, pl.ds(8 * tiles + 8, 4) if up else pl.ds(4, 4)]
             step_x = lattice_dirs[q][0]
             if step_x:
-                at = start + 4 * j + (0 if step_x > 0 else 3)
+                at = 4 * j + (0 if step_x > 0 else 3)
                 target[pl.ds(at, 1)] = from_lat(q, up, tiles - 1 if up else 0)
-        target[pl.ds(start + 20, 4)] = jnp.zeros((4, LANES), F32)
-
-    for target, start, flag in (
-        ((up_msg, base, next_upper), (pair_msg, 0, is_upper))
-        if level == 0
-        else ((up_msg, base, next_upper),)
-    ):
-
-        @pl.when(jnp.logical_not(flag))
-        def _(target=target, start=start):
-            faces(target, start, z_plus)
-
-        @pl.when(flag)
-        def _(target=target, start=start):
-            faces(target, start, z_minus)
-
-
-def spread_kernel(moved, even_got, odd_got, after, out_hbm, tops, patched, sems, *, tiles):
-    del after
-    lat, lats = lax.axis_index("lat"), lax.axis_size("lat")
-    odd_lat = lax.rem(lat, 2) == 1
-    body = pl.ds(8, 8 * tiles)
-    copies = []
-    for q in range(DIRS):
-        if lattice_dirs[q][0] == 0:
-            copies.append(pltpu.make_async_copy(moved.at[q, body], out_hbm.at[q], sems.at[q]))
-            copies[-1].start()
-    order = {q: j for j, q in enumerate(x_plus + x_minus)}
-
-    def fill(dirs, got, keep):
-        for j, q in enumerate(dirs):
-            for k in range(tiles + 2):
-                patched[order[q], pl.ds(8 * k, 8)] = moved[q, pl.ds(8 * k, 8)]
-            even_z = got[pl.ds(2 * tiles * j, tiles)]
-            odd_z = got[pl.ds(2 * tiles * j + tiles, tiles)]
-            patched[order[q], pl.ds(out_odd(q), tiles, stride=8)] = jnp.where(keep, even_z, 0.0)
-            patched[order[q], pl.ds(out_even(q), tiles, stride=8)] = jnp.where(keep, odd_z, 0.0)
-
-    @pl.when(odd_lat)
-    def _():
-        fill(x_plus, even_got, lat > 0)
-        fill(x_minus, odd_got, lat < lats - 1)
-
-    @pl.when(jnp.logical_not(odd_lat))
-    def _():
-        fill(x_plus, odd_got, lat > 0)
-        fill(x_minus, even_got, lat < lats - 1)
-
-    for q in x_plus + x_minus:
-        copies.append(
-            pltpu.make_async_copy(patched.at[order[q], body], out_hbm.at[q], sems.at[q])
-        )
-        copies[-1].start()
-    for j, q in enumerate(z_plus + z_minus):
-        rows = pl.ds(8, 8) if lattice_dirs[q][2] > 0 else pl.ds(8 * tiles, 8)
-        tops[pl.ds(8 * j, 8)] = patched[order[q], rows] if q in order else moved[q, rows]
-    for copy in copies:
-        copy.wait()
-
-
-def finish_kernel(*refs, rows, tiles, levels):
-    it = iter(refs)
-    owns = [next(it) for _ in range(levels)]
-    gots = [next(it) for _ in range(levels)]
-    pair_got, offset, edge, link, tops, pops_in = [next(it) for _ in range(6)]
-    pops_out, conc_out, solved, tiles_out, sems = [next(it) for _ in range(5)]
-    del pops_in
+        target[pl.ds(20, 4)] = jnp.zeros((4, LANES), F32)
+
+    for r, target in enumerate(targets):
+        pl.when(bit(wall, r) == 0)(functools.partial(fill, target, z_plus))
+        pl.when(bit(wall, r) == 1)(functools.partial(fill, target, z_minus))
+
+
+def solve_ions(owns, gots, offset, edge, link, solved, write, *, rows):
+    levels = len(owns)
     wall = lax.axis_index("wall")
-    copies = []
-    for j in range(len(z_plus) + len(z_minus)):
-        tiles_out[pl.ds(8 * j, 8)] = tops[pl.ds(8 * j, 8)]
-
-    def put(got, base, lower):
-        for j in range(5):
-            row = 8 * j if lower else 8 * (5 + j) + 4
-            tiles_out[pl.ds(row, 4)] = got[pl.ds(base + 4 * j, 4)]
-
-    pl.when(bit(wall, 0) == 1)(lambda: put(pair_got, 0, True))
-    pl.when(bit(wall, 0) == 0)(lambda: put(pair_got, 0, False))
-    for r in range(1, levels):
-        base = 32 if r == levels - 1 else 96
-        rest = lax.rem(wall, 2 ** (r + 1))
-        pl.when(rest == 2**r)(functools.partial(put, gots[r], base, True))
-        pl.when(rest == 2**r - 1)(functools.partial(put, gots[r], base, False))
-    for j, q in enumerate(z_plus + z_minus):
-        at = pl.ds(0, 8) if lattice_dirs[q][2] > 0 else pl.ds(8 * tiles - 8, 8)
-        copies.append(
-            pltpu.make_async_copy(tiles_out.at[pl.ds(8 * j, 8)], pops_out.at[q, at], sems.at[j])
-        )
-        copies[-1].start()
     half = rows // 2
     inner = []
     for h in range(2):
@@ -502,30 +422,99 @@
         solved[at0] = u0
         solved[at1] = u1
         inner.append([u0, u1, w_low, w_high])
-    parts = 2
-    step = half // parts
-    for part in range(parts):
-        for i in range(part * step, (part + 1) * step):
-            if i == 0:
-                continue
-            for h in range(2):
-                u0, u1, w_low, w_high = inner[h]
-                at0 = pl.ds(16 * (half - 1 - i) + 8 * h, 8)
-                at1 = pl.ds(16 * (half + i) + 8 * h, 8)
-                u0 = (offset[at0] + edge[at0] * w_low) + link[at0] * u0
-                u1 = (offset[at1] + edge[at1] * w_high) + link[at1] * u1
-                solved[at0] = u0
-                solved[at1] = u1
-                inner[h] = [u0, u1, w_low, w_high]
-        for side in range(2):
-            begin = half - (part + 1) * step if side == 0 else half + part * step
-            span = pl.ds(16 * begin, 16 * step)
-            copies.append(
-                pltpu.make_async_copy(
-                    solved.at[span], conc_out.at[span], sems.at[10 + 2 * part + side]
-                )
-            )
-            copies[-1].start()
+    for i in range(1, half):
+        for h in range(2):
+            u0, u1, w_low, w_high = inner[h]
+            at0 = pl.ds(16 * (half - 1 - i) + 8 * h, 8)
+            at1 = pl.ds(16 * (half + i) + 8 * h, 8)
+            u0 = (offset[at0] + edge[at0] * w_low) + link[at0] * u0
+            u1 = (offset[at1] + edge[at1] * w_high) + link[at1] * u1
+            solved[at0] = u0
+            solved[at1] = u1
+            inner[h] = [u0, u1, w_low, w_high]
+        if i == half // 2 - 1:
+            write(0, half - half // 2, 2 * (half // 2))
+    write(1, 0, half - half // 2)
+    write(2, half + half // 2, half - half // 2)
+
+
+def outputs_kernel(*refs, rows, tiles, levels):
+    it = iter(refs)
+    owns = [next(it) for _ in range(levels)]
+    gots = [next(it) for _ in range(levels)]
+    offset, edge, link, moved, even_got, odd_got, _ = [next(it) for _ in range(7)]
+    pops_out, conc_out, tops, patched, solved, sems = [next(it) for _ in range(6)]
+    lat, lats = lax.axis_index("lat"), lax.axis_size("lat")
+    odd_lat = lax.rem(lat, 2) == 1
+    body = pl.ds(8, 8 * tiles)
+    copies = []
+
+    def start(source, target):
+        copies.append(pltpu.make_async_copy(source, target, sems.at[len(copies)]))
+        copies[-1].start()
+
+    for q in range(DIRS):
+        if lattice_dirs[q][0] == 0:
+            start(moved.at[q, body], pops_out.at[q])
+    order = {q: j for j, q in enumerate(x_plus + x_minus)}
+
+    def fill(dirs, got, keep):
+        for j, q in enumerate(dirs):
+            for k in range(tiles + 2):
+                patched[order[q], pl.ds(8 * k, 8)] = moved[q, pl.ds(8 * k, 8)]
+            even_z = got[pl.ds(2 * tiles * j, tiles)]
+            odd_z = got[pl.ds(2 * tiles * j + tiles, tiles)]
+            patched[order[q], pl.ds(out_odd(q), tiles, stride=8)] = jnp.where(keep, even_z, 0.0)
+            patched[order[q], pl.ds(out_even(q), tiles, stride=8)] = jnp.where(keep, odd_z, 0.0)
+
+    @pl.when(odd_lat)
+    def _():
+        fill(x_plus, even_got, lat > 0)
+        fill(x_minus, odd_got, lat < lats - 1)
+
+    @pl.when(jnp.logical_not(odd_lat))
+    def _():
+        fill(x_plus, odd_got, lat > 0)
+        fill(x_minus, even_got, lat < lats - 1)
+
+    for q in x_plus + x_minus:
+        start(patched.at[order[q], body], pops_out.at[q])
+    for j, q in enumerate(z_plus + z_minus):
+        at = pl.ds(8, 8) if lattice_dirs[q][2] > 0 else pl.ds(8 * tiles, 8)
+        tops[pl.ds(8 * j, 8)] = patched[order[q], at] if q in order else moved[q, at]
+
+    def write(_, begin, count):
+        span = pl.ds(16 * begin, 16 * count)
+        start(solved.at[span], conc_out.at[span])
+
+    solve_ions(owns, gots, offset, edge, link, solved, write, rows=rows)
+    for copy in copies:
+        copy.wait()
+
+
+def patch_kernel(*refs, tiles, levels):
+    gots = refs[:levels]
+    tops, _, pops_out, fixed, sems = refs[levels:]
+    wall = lax.axis_index("wall")
+    for j in range(len(z_plus) + len(z_minus)):
+        fixed[pl.ds(8 * j, 8)] = tops[pl.ds(8 * j, 8)]
+
+    def put(got, lower):
+        for j in range(5):
+            row = 8 * j if lower else 8 * (5 + j) + 4
+            fixed[pl.ds(row, 4)] = got[pl.ds(4 * j, 4)]
+
+    for r in range(levels):
+        rest = lax.rem(wall, 2 ** (r + 1))
+        pl.when(rest == 2**r)(functools.partial(put, gots[r], True))
+        pl.when(rest == 2**r - 1)(functools.partial(put, gots[r], False))
+    copies = []
+    for j, q in enumerate(z_plus + z_minus):
+        at = pl.ds(0, 8) if lattice_dirs[q][2] > 0 else pl.ds(8 * tiles - 8, 8)
+        copies.append(
+            pltpu.make_async_copy(fixed.at[pl.ds(8 * j, 8)], pops_out.at[q, at], sems.at[j])
+        )
+        copies[-1].start()
     for copy in copies:
         copy.wait()
 
@@ -582,11 +571,12 @@
         in_specs=[ANY_SPEC] * 6,
         out_specs=(VMEM_SPEC,) * 7,
         scratch_shapes=[
-            pltpu.VMEM((DIRS, cells, LANES), F32),
+            pltpu.VMEM((DIRS + SPECIES, cells, LANES), F32),
+            pltpu.VMEM((10, cells, LANES), F32),
             pltpu.SMEM((SPECIES,), jnp.int32),
             pltpu.SMEM((SPECIES,), F32),
             pltpu.SMEM((3,), F32),
-            pltpu.SemaphoreType.DMA((4 + 2 * len(chunks),)),
+            pltpu.SemaphoreType.DMA((4 + len(chunks),)),
         ],
         compiler_params=params(),
         cost_estimate=cost(5_000_000, 3_000_000),
@@ -601,7 +591,8 @@
             applied_field,
         )
     )
-    even_got, odd_got = move(even_msg, even), move(odd_msg, odd)
+    odd_got = move(odd_msg, odd)
+    even_got = move(even_msg, even)
 
     offset, edge, link, ends = pl.pallas_call(
         functools.partial(eliminate_kernel, rows=rows),
@@ -613,63 +604,67 @@
         name="eliminate",
     )(*pin(vel_z, conc, flags, table))
 
+    depth = len(levels)
     owns, gots = [ends], [move(ends, levels[0])]
-    pair_got = None
-    for level in range(len(levels) - 1):
-        last = level == len(levels) - 2
-        shapes = (on_chip((32 if last else 96) + FACE_ROWS, LANES),)
-        if level == 0:
-            shapes += (on_chip(FACE_ROWS, LANES),)
+    for level in range(depth - 1):
+        last = level == depth - 2
         sent = pl.pallas_call(
-            functools.partial(relay_kernel, tiles=tiles, level=level, last=last),
-            out_shape=shapes,
-            in_specs=[VMEM_SPEC] * 5,
-            out_specs=(VMEM_SPEC,) * len(shapes),
+            functools.partial(relay_kernel, level=level, last=last),
+            out_shape=on_chip(32 if last else 96, LANES),
+            in_specs=[VMEM_SPEC] * 2,
+            out_specs=VMEM_SPEC,
             compiler_params=params(),
             cost_estimate=cost(100_000, 200_000),
             name=f"relay{level}",
-        )(*pin(owns[-1], gots[-1], moved, even_got, odd_got))
-        owns.append(sent[0])
-        gots.append(move(sent[0], levels[level + 1]))
-        if level == 0:
-            pair_got = move(sent[1], levels[0])
-
-    pops_out, tops = pl.pallas_call(
-        functools.partial(spread_kernel, tiles=tiles),
+        )(*pin(owns[-1], gots[-1]))
+        owns.append(sent)
+        gots.append(move(sent, levels[level + 1]))
+
+    faces = pl.pallas_call(
+        functools.partial(faces_kernel, tiles=tiles),
+        out_shape=(on_chip(FACE_ROWS, LANES),) * depth,
+        in_specs=[VMEM_SPEC] * 3,
+        out_specs=(VMEM_SPEC,) * depth,
+        compiler_params=params(),
+        cost_estimate=cost(100_000, 200_000),
+        name="faces",
+    )(*pin(moved, even_got, odd_got))
+    face_gots = [move(face, table) for face, table in zip(faces, levels)]
+
+    operands = pin(*owns, *gots, offset, edge, link, moved, even_got, odd_got, faces[-1])
+    pops_out, new_conc, tops = pl.pallas_call(
+        functools.partial(outputs_kernel, rows=rows, tiles=tiles, levels=depth),
         out_shape=(
             jax.ShapeDtypeStruct((DIRS, cells, LANES), F32),
+            jax.ShapeDtypeStruct((cells * SPECIES, LANES), F32),
             on_chip(80, LANES),
         ),
-        in_specs=[VMEM_SPEC] * 4,
-        out_specs=(ANY_SPEC, VMEM_SPEC),
+        in_specs=[VMEM_SPEC] * len(operands),
+        out_specs=(ANY_SPEC, ANY_SPEC, VMEM_SPEC),
         scratch_shapes=[
             pltpu.VMEM((10, cells + 16, LANES), F32),
-            pltpu.SemaphoreType.DMA((DIRS,)),
+            pltpu.VMEM((cells * SPECIES, LANES), F32),
+            pltpu.SemaphoreType.DMA((DIRS + 3,)),
         ],
         compiler_params=params(),
         cost_estimate=cost(1_000_000, 2_500_000),
-        name="spread",
-    )(*pin(moved, even_got, odd_got, owns[-1]))
-
-    n_in = 2 * len(levels) + 5
-    new_pops, new_conc = pl.pallas_call(
-        functools.partial(finish_kernel, rows=rows, tiles=tiles, levels=len(levels)),
-        out_shape=(
-            jax.ShapeDtypeStruct((DIRS, cells, LANES), F32),
-            jax.ShapeDtypeStruct((cells * SPECIES, LANES), F32),
-        ),
-        in_specs=[VMEM_SPEC] * n_in + [ANY_SPEC],
-        out_specs=(ANY_SPEC, ANY_SPEC),
-        input_output_aliases={n_in: 0},
+        name="outputs",
+    )(*operands)
+
+    new_pops = pl.pallas_call(
+        functools.partial(patch_kernel, tiles=tiles, levels=depth),
+        out_shape=jax.ShapeDtypeStruct((DIRS, cells, LANES), F32),
+        in_specs=[VMEM_SPEC] * (depth + 1) + [ANY_SPEC],
+        out_specs=ANY_SPEC,
+        input_output_aliases={depth + 1: 0},
         scratch_shapes=[
-            pltpu.VMEM((cells * SPECIES, LANES), F32),
             pltpu.VMEM((80, LANES), F32),
-            pltpu.SemaphoreType.DMA((14,)),
+            pltpu.SemaphoreType.DMA((10,)),
         ],
         compiler_params=params(),
-        cost_estimate=cost(1_000_000, 2_000_000),
-        name="finish",
-    )(*pin(*owns, *gots, pair_got, offset, edge, link, tops), pops_out)
+        cost_estimate=cost(10_000, 100_000),
+        name="patch",
+    )(*pin(*face_gots, tops), pops_out)
     return new_pops.reshape(populations.shape), new_conc.reshape(concentration.shape)
 
 

time: 14.5 us -> 13.9 us (0.959)
  waiting for transfers between devices: 3.7 us -> 1.37 us
  starting transfers between devices: 5.62 us -> 7.49 us
    ppermute x5 -> x6, waiting for transfers between devices: 3.7 us -> 1.37 us  [move(): return lax.ppermute(x, ('lat', 'wall'), table)]
    ppermute x5 -> x6, starting transfers between devices: 5.62 us -> 7.49 us  [move(): return lax.ppermute(x, ('lat', 'wall'), table)]
    pallas_call x3 -> x4, Pallas kernels: 2.09 us -> 2.06 us  [the longest x1 1.29 us: per_device(): pl.pallas_call(functools.partial(outputs_kernel, rows=rows, tiles=tiles,...]
  transfers between devices with their start and end apart: 5 -> 6, of which waited for: 3 -> 3; matrix products, arithmetic and copies ran while one was open for 0% -> 0% of each run, Pallas kernels for 10% -> 12%
where the time goes in v2:
time: 13.9 us; the launch traced here: 13.8 us
  starting transfers between devices  7.49 us (54%)
  Pallas kernels  4.26 us (31%)
  waiting for transfers between devices  1.37 us (10%)
  between operations  0.67 us (5%)
    ppermute x6, starting transfers between devices, move(): return lax.ppermute(x, ('lat', 'wall'), table)  7.49 us
    pallas_call x1, Pallas kernels, per_device(): pl.pallas_call(functools.partial(collide_kernel, chunks=chunks), out_shap...  1.88 us
    ppermute x6, waiting for transfers between devices, move(): return lax.ppermute(x, ('lat', 'wall'), table)  1.37 us
    pallas_call x1, Pallas kernels, per_device(): pl.pallas_call(functools.partial(outputs_kernel, rows=rows, tiles=tiles,...  1.29 us
    pallas_call x1, Pallas kernels, per_device(): pl.pallas_call(functools.partial(patch_kernel, tiles=tiles, levels=depth)...  0.73 us
    pallas_call x1, Pallas kernels, per_device(): pl.pallas_call(functools.partial(eliminate_kernel, rows=rows), out_shape=...  0.32 us
  transfers between devices with their start and end apart: 6, of which 3 were waited for; matrix products, arithmetic and copies ran while one was open for 0% of the time, Pallas kernels for 12%

profile of v2, /device:TPU:9, one launch (start us, length us, event | category | flops | bytes accessed | tf_op | source)
XLA Modules:
  0.0 13.8 jit_solution(2311311421887933398)
XLA Ops:
  0.6 1.9 %collide.1 = (f32[19,144,128]{2,1,0:T(8,128)S(1)}, f32[160,128]{1,0:T(8,128)S(1)}, f32[160,128]{1,0:T(8,128)S(1)}, f32[128,128]{1,0:T(8,128)S(1)}, f32[512,128]{...) custom-call(f32[19,128,128]{2,1,0:T(8,128)} %bitcast.5, f32[512,128]{1,0:T(8,128)} %bitcast.7, ...), custom_call_target="tpu_custom_call" | custom-call | flops 5000000 | bytes 3000000 | tf_op jit(solution)/shard_map/collide/pallas_call | solution.py:560
  2.5 1.3 %collective-permute-start = (f32[160,128]{1,0:T(8,128)S(1)}, f32[160,128]{1,0:T(8,128)S(1)}, u32[]{:S(2)}, u32[]{:S(2)}) collective-permute-start(f32[160,128]{1,0:T(8,128)S(1)} %get-tuple-element.19), channel_id=1, source_target_pairs={{0,4},{1,5},{2,6},{3,7},{4,0},{5,1},{6,2},{7,3},{8,12},{9,13},{10,... | collective-permute-start | bytes 245768 | tf_op jit(solution)/shard_map/ppermute | solution.py:557
  3.9 0.0 collective-permute-start.1
  3.9 0.3 %eliminate.1 = (f32[512,128]{1,0:T(8,128)S(1)}, f32[512,128]{1,0:T(8,128)S(1)}, f32[512,128]{1,0:T(8,128)S(1)}, f32[96,128]{1,0:T(8,128)S(1)}) custom-call(f32[128,128]{1,0:T(8,128)S(1)} %get-tuple-element.23.vel_z, f32[512,128]{1,0:T(8,128)S(1)} %get-tuple-element.24.conc, s32[128,128]{1,0:T(8,128)S(1)} %get-tuple-element.25.flags, ...), custom_call_target="tpu_custom_call" | custom-call | flops 5000000 | bytes 3000000 | tf_op jit(solution)/shard_map/eliminate/pallas_call | solution.py:597
  4.2 1.0 %collective-permute-start.4 = (f32[96,128]{1,0:T(8,128)S(1)}, f32[96,128]{1,0:T(8,128)S(1)}, u32[]{:S(2)}, u32[]{:S(2)}) collective-permute-start(f32[96,128]{1,0:T(8,128)S(1)} %get-tuple-element.27.own.refs_0_), channel_id=1, source_target_pairs={{0,1},{1,0},{2,3},{3,2},{4,5},{5,4},{6,7},{7,6},{8,9},{9,8},{10,11... | collective-permute-start | bytes 147464 | tf_op jit(solution)/shard_map/ppermute | solution.py:557
  5.2 0.9 %collective-permute-done.4.got.refs_2_ = f32[96,128]{1,0:T(8,128)S(1)} collective-permute-done((f32[96,128]{1,0:T(8,128)S(1)}, f32[96,128]{1,0:T(8,128)S(1)}, u32[]{:S(2)}, u32[]{:S(2)}) %collective-permute-start.4) | collective-permute-done | bytes 49184 | tf_op jit(solution)/shard_map/ppermute | solution.py:557
  6.1 1.9 %collective-permute-start.5 = (f32[32,128]{1,0:T(8,128)S(1)}, f32[32,128]{1,0:T(8,128)S(1)}, u32[]{:S(2)}, u32[]{:S(2)}) collective-permute-start(f32[32,128]{1,0:T(8,128)S(1)} %relay0.1.refs_1_), channel_id=1, source_target_pairs={{0,3},{1,2},{2,1},{3,0},{4,7},{5,6},{6,5},{7,4},{8,11},{9,10},{10,... | collective-permute-start | bytes 49160 | tf_op jit(solution)/shard_map/ppermute | solution.py:557
  8.0 0.0 collective-permute-done.even_got.refs_8_
  8.0 0.1 collective-permute-done.1.odd_got.refs_9_
  8.1 3.3 %collective-permute-start.3 = (f32[24,128]{1,0:T(8,128)S(1)}, f32[24,128]{1,0:T(8,128)S(1)}, u32[]{:S(2)}, u32[]{:S(2)}) collective-permute-start(f32[24,128]{1,0:T(8,128)S(1)} %get-tuple-element.22.refs_10_), channel_id=1, source_target_pairs={{0,3},{1,2},{2,1},{3,0},{4,7},{5,6},{6,5},{7,4},{8,11},{9,10},{10,... | collective-permute-start | bytes 36872 | tf_op jit(solution)/shard_map/ppermute | solution.py:557
  11.3 0.0 collective-permute-start.2
  11.3 0.0 collective-permute-done.5.refs_3_
  11.3 1.3 %outputs.1 = (f32[19,128,128]{2,1,0:T(8,128)}, f32[512,128]{1,0:T(8,128)}, f32[80,128]{1,0:T(8,128)S(1)}) custom-call(f32[96,128]{1,0:T(8,128)S(1)} %get-tuple-element.27.own.refs_0_, f32[32,128]{1,0:T(8,128)S(1)} %relay0.1.refs_1_, f32[96,128]{1,0:T(8,128)S(1)} %collective-permute-done.4.got.refs_2_, f32[32,128]{1,0:T(8,128)S(1)} %collective-permute-done.5.refs_3_, ...), custom_call_target="tpu_custom_call" | custom-call | flops 1000000 | bytes 2500000 | tf_op jit(solution)/shard_map/outputs/pallas_call | solution.py:635
  12.6 0.4 %collective-permute-done.3.refs_1_ = f32[24,128]{1,0:T(8,128)S(1)} collective-permute-done((f32[24,128]{1,0:T(8,128)S(1)}, f32[24,128]{1,0:T(8,128)S(1)}, u32[]{:S(2)}, u32[]{:S(2)}) %collective-permute-start.3) | collective-permute-done | bytes 12320 | tf_op jit(solution)/shard_map/ppermute | solution.py:557
  13.1 0.0 collective-permute-done.2.refs_0_
  13.1 0.7 %patch.1 = f32[19,128,128]{2,1,0:T(8,128)} custom-call(f32[24,128]{1,0:T(8,128)S(1)} %collective-permute-done.2.refs_0_, f32[24,128]{1,0:T(8,128)S(1)} %collective-permute-done.3.refs_1_, f32[80,128]{1,0:T(8,128)S(1)} %get-tuple-element.31.refs_2_, f32[19,128,128]{2,1,0:T(8,128)} %get-tuple-element.32.refs_3_), custom_call_target="tpu_custom_call", output_to_operand_aliasing={{}: (3, {})} | custom-call | flops 10000 | bytes 100000 | tf_op jit(solution)/shard_map/patch/pallas_call | solution.py:654
  (2 shorter events, 0.0 us)
Async XLA Ops:
  2.5 5.5 %collective-permute-start = (f32[160,128]{1,0:T(8,128)S(1)}, f32[160,128]{1,0:T(8,128)S(1)}, u32[]{:S(2)}, u32[]{:S(2)}) collective-permute-start(f32[160,128]{1,0:T(8,128)S(1)} %get-tuple-element.19), channel_id=1, source_target_pairs={{0,4},{1,5},{2,6},{3,7},{4,0},{5,1},{6,2},{7,3},{8,12},{9,13},{10,... | collective-permute-start | bytes 245768 | tf_op jit(solution)/shard_map/ppermute | solution.py:557
  3.9 4.2 %collective-permute-start.1 = (f32[160,128]{1,0:T(8,128)S(1)}, f32[160,128]{1,0:T(8,128)S(1)}, u32[]{:S(2)}, u32[]{:S(2)}) collective-permute-start(f32[160,128]{1,0:T(8,128)S(1)} %get-tuple-element.20), channel_id=1, source_target_pairs={{0,1},{1,0},{2,3},{3,2},{4,8},{5,9},{6,10},{7,11},{8,4},{9,5},{10,... | collective-permute-start | bytes 245768 | tf_op jit(solution)/shard_map/ppermute | solution.py:557
  4.2 1.9 %collective-permute-start.4 = (f32[96,128]{1,0:T(8,128)S(1)}, f32[96,128]{1,0:T(8,128)S(1)}, u32[]{:S(2)}, u32[]{:S(2)}) collective-permute-start(f32[96,128]{1,0:T(8,128)S(1)} %get-tuple-element.27.own.refs_0_), channel_id=1, source_target_pairs={{0,1},{1,0},{2,3},{3,2},{4,5},{5,4},{6,7},{7,6},{8,9},{9,8},{10,11... | collective-permute-start | bytes 147464 | tf_op jit(solution)/shard_map/ppermute | solution.py:557
  6.1 5.2 %collective-permute-start.5 = (f32[32,128]{1,0:T(8,128)S(1)}, f32[32,128]{1,0:T(8,128)S(1)}, u32[]{:S(2)}, u32[]{:S(2)}) collective-permute-start(f32[32,128]{1,0:T(8,128)S(1)} %relay0.1.refs_1_), channel_id=1, source_target_pairs={{0,3},{1,2},{2,1},{3,0},{4,7},{5,6},{6,5},{7,4},{8,11},{9,10},{10,... | collective-permute-start | bytes 49160 | tf_op jit(solution)/shard_map/ppermute | solution.py:557
  8.1 5.0 %collective-permute-start.3 = (f32[24,128]{1,0:T(8,128)S(1)}, f32[24,128]{1,0:T(8,128)S(1)}, u32[]{:S(2)}, u32[]{:S(2)}) collective-permute-start(f32[24,128]{1,0:T(8,128)S(1)} %get-tuple-element.22.refs_10_), channel_id=1, source_target_pairs={{0,3},{1,2},{2,1},{3,0},{4,7},{5,6},{6,5},{7,4},{8,11},{9,10},{10,... | collective-permute-start | bytes 36872 | tf_op jit(solution)/shard_map/ppermute | solution.py:557
  11.3 1.7 %collective-permute-start.2 = (f32[24,128]{1,0:T(8,128)S(1)}, f32[24,128]{1,0:T(8,128)S(1)}, u32[]{:S(2)}, u32[]{:S(2)}) collective-permute-start(f32[24,128]{1,0:T(8,128)S(1)} %get-tuple-element.21), channel_id=1, source_target_pairs={{0,1},{1,0},{2,3},{3,2},{4,5},{5,4},{6,7},{7,6},{8,9},{9,8},{10,11... | collective-permute-start | bytes 36872 | tf_op jit(solution)/shard_map/ppermute | solution.py:557

commit v3 on v2

--- a/solution.py
+++ b/solution.py
@@ -79,22 +79,63 @@
     return lax.broadcasted_iota(jnp.int32, (8, LANES), 0) < 4
 
 
-def collide_kernel(
+def density_and_momentum(p):
+    diff = {q: p[q] - p[q + 1] for q in range(1, DIRS, 2)}
+    total = {q: p[q] + p[q + 1] for q in range(1, DIRS, 2)}
+    density = (
+        ((p[0] + total[1]) + (total[3] + total[5]))
+        + ((total[7] + total[9]) + (total[11] + total[13]))
+        + (total[15] + total[17])
+    )
+    momentum = [
+        (diff[1] + diff[7]) + (diff[9] + diff[11]) + diff[13],
+        (diff[3] + diff[7]) - (diff[9] - diff[15]) + diff[17],
+        (diff[5] + diff[11]) - (diff[13] - diff[15]) - diff[17],
+    ]
+    return density, momentum
+
+
+def moments(p, charge, field_xyz):
+    density, momentum = density_and_momentum(p)
+    force = [charge * f for f in field_xyz]
+    inverse = 1.0 / density
+    vel = [(momentum[a] + 0.5 * force[a]) * inverse for a in range(3)]
+    speed_sq = vel[0] * vel[0] + vel[1] * vel[1] + vel[2] * vel[2]
+    work = vel[0] * force[0] + vel[1] * force[1] + vel[2] * force[2]
+    base = (1.25 / 36.0 * density) * (1.0 - 1.5 * speed_sq) - (1.125 / 36.0) * work
+    odd = [(3.75 / 36.0) * momentum[a] + (3.0 / 36.0) * force[a] for a in range(3)]
+    even = [(5.625 / 36.0) * momentum[a] + (6.1875 / 36.0) * force[a] for a in range(3)]
+    return base, vel, odd, even
+
+
+def parts_of(q, base, vel, odd, even):
+    axes = [(a, lattice_dirs[q][a]) for a in range(3) if lattice_dirs[q][a]]
+
+    def along(v):
+        out = v[axes[0][0]]
+        for a, sign in axes[1:]:
+            out = out + v[a] if sign > 0 else out - v[a]
+        return out
+
+    cu, odd_q, even_q = along(vel), along(odd), along(even)
+    if len(axes) == 1:
+        return (base + base) + 2.0 * (cu * even_q), odd_q + odd_q
+    return base + cu * even_q, odd_q
+
+
+def edges_kernel(
     pops_hbm,
     conc_hbm,
     flags_hbm,
     valence_hbm,
     diffusivity_hbm,
     field_hbm,
-    moved,
     even_msg,
     odd_msg,
-    vel_z,
+    pops,
     conc,
     flags,
     table,
-    pops,
-    mid,
     valence,
     diffusivity,
     field,
@@ -102,7 +143,6 @@
     *,
     chunks,
 ):
-    tiles = sum(chunks)
     small = [
         pltpu.make_async_copy(source, target, sems.at[i])
         for i, (source, target) in enumerate(
@@ -116,85 +156,73 @@
     ]
     for copy in small:
         copy.start()
-    copies = {}
+    arrived = {}
     at = 0
     for c, count in enumerate(chunks):
-        rows = pl.ds(8 * at, 8 * count)
-        crows = pl.ds(8 * SPECIES * at, 8 * SPECIES * count)
-        copies[at] = (
-            pltpu.make_async_copy(conc_hbm.at[crows], conc.at[crows], sems.at[4 + c]),
-            pltpu.make_async_copy(
-                pops_hbm.at[:, rows], pops.at[pl.ds(0, DIRS), rows], sems.at[4 + c]
-            ),
-        )
-        for copy in copies[at]:
-            copy.start()
+        rows = pl.ds(32 * at, 32 * count)
+        crows = pl.ds(128 * at, 128 * count)
+        sem = sems.at[4 + c]
+        pltpu.make_async_copy(conc_hbm.at[crows], conc.at[crows], sem).start()
+        pltpu.make_async_copy(pops_hbm.at[:, rows], pops.at[pl.ds(0, DIRS), rows], sem).start()
         both = pops.at[:, rows]
-        copies[at] = pltpu.make_async_copy(both, both, sems.at[4 + c])
+        arrived[at] = pltpu.make_async_copy(both, both, sem)
         at += count
     low = low_rows()
     for copy in small:
         copy.wait()
-    val_pair = [
-        jnp.where(low, valence[2 * h].astype(F32), valence[2 * h + 1].astype(F32))
-        for h in range(2)
-    ]
+    val = [valence[s].astype(F32) for s in range(SPECIES)]
     field_xyz = [FORCE_GAIN * field[axis] for axis in range(3)]
-
-    def moments(at):
-        p = [pops[q, pl.ds(at, 8)] for q in range(DIRS)]
-        sums = []
-        for z in range(2):
-            part = val_pair[0] * conc[pl.ds(4 * at + 16 * z, 8)]
-            part = part + val_pair[1] * conc[pl.ds(4 * at + 16 * z + 8, 8)]
-            sums.append(part + pltpu.roll(part, 4, axis=0))
-        charge = jnp.where(low, sums[0], sums[1])
-        diff = {q: p[q] - p[q + 1] for q in range(1, DIRS, 2)}
-        total = {q: p[q] + p[q + 1] for q in range(1, DIRS, 2)}
-        density = (
-            ((p[0] + total[1]) + (total[3] + total[5]))
-            + ((total[7] + total[9]) + (total[11] + total[13]))
-            + (total[15] + total[17])
-        )
-        momentum = [
-            (diff[1] + diff[7]) + (diff[9] + diff[11]) + diff[13],
-            (diff[3] + diff[7]) - (diff[9] - diff[15]) + diff[17],
-            (diff[5] + diff[11]) - (diff[13] - diff[15]) - diff[17],
+    values = [jnp.full((8, LANES), f, F32) for f in field_xyz]
+    for h in range(2):
+        diff = jnp.where(low, diffusivity[2 * h], diffusivity[2 * h + 1])
+        val_pair = jnp.where(low, val[2 * h], val[2 * h + 1])
+        values += [
+            val_pair,
+            diff,
+            diff * 0.01,
+            diff * jnp.where(val_pair > 0, 0.5, 0.02),
+            val_pair * field[2],
         ]
-        force = [charge * f for f in field_xyz]
-        inverse = 1.0 / density
-        vel = [(momentum[a] + 0.5 * force[a]) * inverse for a in range(3)]
-        vel_z[pl.ds(at, 8)] = vel[2]
-        speed_sq = vel[0] * vel[0] + vel[1] * vel[1] + vel[2] * vel[2]
-        work = vel[0] * force[0] + vel[1] * force[1] + vel[2] * force[2]
-        base = (1.25 / 36.0 * density) * (1.0 - 1.5 * speed_sq) - (1.125 / 36.0) * work
-        odd = [(3.75 / 36.0) * momentum[a] + (3.0 / 36.0) * force[a] for a in range(3)]
-        even = [(5.625 / 36.0) * momentum[a] + (6.1875 / 36.0) * force[a] for a in range(3)]
-        for j, value in enumerate((base, *vel, *odd, *even)):
-            mid[j, pl.ds(at, 8)] = value
-
+    for j, value in enumerate(values):
+        table[pl.ds(8 * j, 8)] = value
+    is_odd = lax.rem(lax.axis_index("lat"), 2) == 1
+    for g in range(sum(chunks)):
+        if g in arrived:
+            arrived[g].wait()
+        sent = {}
+        for x, dirs in ((X_CELLS - 1, x_plus), (0, x_minus)):
+            at = pl.ds(32 * g + x, 8, stride=4)
+            p = [pops[q, at] for q in range(DIRS)]
+            solid = flags[at] != 0
+            terms = [
+                val[s] * conc[pl.ds(128 * g + 4 * s + x, 8, stride=16)] for s in range(SPECIES)
+            ]
+            charge = (terms[0] + terms[1]) + (terms[2] + terms[3])
+            found = moments(p, charge, field_xyz)
+            for j, q in enumerate(dirs):
+                first = q if q % 2 else q - 1
+                shared, odd = parts_of(first, *found)
+                relaxed = (shared + odd if q % 2 else shared - odd) - 0.25 * p[q]
+                value = jnp.where(solid, p[q + 1 if q % 2 else q - 1], relaxed)
+                step_y = lattice_dirs[q][1]
+                if step_y:
+                    value = pltpu.roll(value, step_y % LANES, axis=1)
+                sent[x, j] = value
+        for j in range(5):
+            plus, minus = sent[X_CELLS - 1, j], sent[0, j]
+            at = pl.ds(8 * sum(chunks) * j + 8 * g, 8)
+            even_msg[at] = jnp.where(is_odd, minus, plus)
+            odd_msg[at] = jnp.where(is_odd, plus, minus)
+
+
+def collide_kernel(pops, flags, mid, moved, *, tiles):
     def scatter(at):
         solid = flags[pl.ds(at, 8)] != 0
-        base36, *rest = [mid[j, pl.ds(at, 8)] for j in range(10)]
-        vel, odd36, even36 = rest[:3], rest[3:6], rest[6:]
-        base18 = base36 + base36
+        base, *rest = [mid[j, pl.ds(at, 8)] for j in range(10)]
         p0 = pops[0, pl.ds(at, 8)]
-        moved[0, pl.ds(8 + at, 8)] = jnp.where(solid, p0, 12.0 * base36 - 0.25 * p0)
+        moved[0, pl.ds(8 + at, 8)] = jnp.where(solid, p0, 12.0 * base - 0.25 * p0)
         for q in range(1, DIRS, 2):
-            axes = [(a, lattice_dirs[q][a]) for a in range(3) if lattice_dirs[q][a]]
-
-            def along(v):
-                out = v[axes[0][0]]
-                for a, sign in axes[1:]:
-                    out = out + v[a] if sign > 0 else out - v[a]
-                return out
-
-            cu, odd, even = along(vel), along(odd36), along(even36)
-            if len(axes) == 1:
-                shared = base18 + 2.0 * (cu * even)
-                odd = odd + odd
-            else:
-                shared = base36 + cu * even
+            shared, odd = parts_of(q, base, rest[:3], rest[3:6], rest[6:])
             ahead, behind = pops[q, pl.ds(at, 8)], pops[q + 1, pl.ds(at, 8)]
             for d, relaxed, bounced in (
                 (q, (shared + odd) - 0.25 * ahead, behind),
@@ -208,64 +236,43 @@
                     value = pltpu.roll(value, step_x % 8, axis=0)
                 moved[d, pl.ds(8 + at + 4 * step_z, 8)] = value
 
-    at = 0
-    for count in chunks:
-        copies[at].wait()
-        for k in range(at, at + count):
-            moments(8 * k)
-        for k in range(at, at + count):
-            scatter(8 * k)
-        at += count
+    for k in range(tiles):
+        scatter(8 * k)
     for d in z_plus + z_minus:
         at = 8 if lattice_dirs[d][2] > 0 else 8 * tiles + 4
         moved[d, pl.ds(at, 4)] = jnp.zeros((4, LANES), F32)
 
-    def pack(target, dirs):
-        for j, q in enumerate(dirs):
-            target[pl.ds(2 * tiles * j, tiles)] = moved[q, pl.ds(out_even(q), tiles, stride=8)]
-            target[pl.ds(2 * tiles * j + tiles, tiles)] = moved[
-                q, pl.ds(out_odd(q), tiles, stride=8)
-            ]
-
-    is_odd = lax.rem(lax.axis_index("lat"), 2) == 1
-
-    @pl.when(jnp.logical_not(is_odd))
-    def _():
-        pack(even_msg, x_plus)
-        pack(odd_msg, x_minus)
-
-    @pl.when(is_odd)
-    def _():
-        pack(even_msg, x_minus)
-        pack(odd_msg, x_plus)
-
-    for h in range(2):
-        diff = jnp.where(low, diffusivity[2 * h], diffusivity[2 * h + 1])
-        values = (
-            diff,
-            diff * 0.01,
-            diff * jnp.where(val_pair[h] > 0, 0.5, 0.02),
-            val_pair[h] * field[2],
-        )
-        for j, value in enumerate(values):
-            table[pl.ds(8 * (4 * h + j), 8)] = value
-
 
 def reciprocal(x):
     return 1.0 / x
 
 
 def eliminate_kernel(
-    vel_z, conc, flags, table, offset, edge, link, ends, *, rows
+    pops, conc, flags, table, mid, offset, edge, link, ends, *, rows
 ):
     low = low_rows()
     half = rows // 2
+    field_xyz = [table[pl.ds(8 * a, 8)] for a in range(3)]
+    val_pair = [table[pl.ds(8 * (3 + 5 * h), 8)] for h in range(2)]
+    for k in range(half):
+        at = 8 * k
+        sums = []
+        for z in range(2):
+            part = val_pair[0] * conc[pl.ds(4 * at + 16 * z, 8)]
+            part = part + val_pair[1] * conc[pl.ds(4 * at + 16 * z + 8, 8)]
+            sums.append(part + pltpu.roll(part, 4, axis=0))
+        charge = jnp.where(low, sums[0], sums[1])
+        base, vel, odd, even = moments(
+            [pops[q, pl.ds(at, 8)] for q in range(DIRS)], charge, field_xyz
+        )
+        for j, value in enumerate((base, *vel, *odd, *even)):
+            mid[j, pl.ds(at, 8)] = value
     for h in range(2):
-        diff, slow, membrane, pull = [table[pl.ds(8 * (4 * h + j), 8)] for j in range(4)]
+        diff, slow, membrane, pull = [table[pl.ds(8 * (4 + 5 * h + j), 8)] for j in range(4)]
 
         def coefficients(z):
             tile = pl.ds(8 * (z // 2), 8)
-            vz, flag = vel_z[tile], flags[tile]
+            vz, flag = mid[3, tile], flags[tile]
             mine = low if z % 2 == 0 else jnp.logical_not(low)
             vz = jnp.where(mine, vz, pltpu.roll(vz, 4, axis=0))
             flag = jnp.where(mine, flag, pltpu.roll(flag, 4, axis=0))
@@ -347,7 +354,7 @@
     return top_a, low_b, merged
 
 
-def relay_kernel(own, got, send, *, level, last):
+def relay_kernel(own, got, _, send, *, level, last):
     wall = lax.axis_index("wall")
     is_upper = bit(wall, level) == 1
     next_upper = bit(wall, level + 1) == 1
@@ -370,7 +377,7 @@
 
     def from_lat(q, odd_z, index):
         dirs = x_plus if q in x_plus else x_minus
-        at = pl.ds(2 * tiles * dirs.index(q) + (tiles if odd_z else 0) + index, 1)
+        at = pl.ds(2 * tiles * dirs.index(q) + 2 * index + (1 if odd_z else 0), 1)
         use_even = odd_lat if q in x_plus else jnp.logical_not(odd_lat)
         exists = lat > 0 if q in x_plus else lat < lats - 1
         row = jnp.where(use_even, even_got[at], odd_got[at])
@@ -462,8 +469,8 @@
         for j, q in enumerate(dirs):
             for k in range(tiles + 2):
                 patched[order[q], pl.ds(8 * k, 8)] = moved[q, pl.ds(8 * k, 8)]
-            even_z = got[pl.ds(2 * tiles * j, tiles)]
-            odd_z = got[pl.ds(2 * tiles * j + tiles, tiles)]
+            even_z = got[pl.ds(2 * tiles * j, tiles, stride=2)]
+            odd_z = got[pl.ds(2 * tiles * j + 1, tiles, stride=2)]
             patched[order[q], pl.ds(out_odd(q), tiles, stride=8)] = jnp.where(keep, even_z, 0.0)
             patched[order[q], pl.ds(out_even(q), tiles, stride=8)] = jnp.where(keep, odd_z, 0.0)
 
@@ -494,7 +501,7 @@
 
 def patch_kernel(*refs, tiles, levels):
     gots = refs[:levels]
-    tops, _, pops_out, fixed, sems = refs[levels:]
+    tops, _, pops_out, fixed, sem = refs[levels:]
     wall = lax.axis_index("wall")
     for j in range(len(z_plus) + len(z_minus)):
         fixed[pl.ds(8 * j, 8)] = tops[pl.ds(8 * j, 8)]
@@ -508,15 +515,10 @@
         rest = lax.rem(wall, 2 ** (r + 1))
         pl.when(rest == 2**r)(functools.partial(put, gots[r], True))
         pl.when(rest == 2**r - 1)(functools.partial(put, gots[r], False))
-    copies = []
     for j, q in enumerate(z_plus + z_minus):
         at = pl.ds(0, 8) if lattice_dirs[q][2] > 0 else pl.ds(8 * tiles - 8, 8)
-        copies.append(
-            pltpu.make_async_copy(fixed.at[pl.ds(8 * j, 8)], pops_out.at[q, at], sems.at[j])
-        )
-        copies[-1].start()
-    for copy in copies:
-        copy.wait()
+        pltpu.make_async_copy(fixed.at[pl.ds(8 * j, 8)], pops_out.at[q, at], sem).start()
+    pltpu.make_async_copy(fixed, fixed, sem).wait()
 
 
 def swaps(lats, walls):
@@ -547,8 +549,7 @@
 ):
     rows, cells = populations.shape[1], populations.shape[1] * populations.shape[2]
     tiles = cells // 8
-    chunks = [tiles // 8, tiles // 4]
-    chunks += [(tiles - sum(chunks)) // 2, (tiles - sum(chunks) + 1) // 2]
+    chunks = [1] * (rows // 8)
     assert populations.shape[2] == X_CELLS and lats % 2 == 0 and walls >= 4
     even, odd, levels = swaps(lats, walls)
     assert 2 ** len(levels) == walls
@@ -557,30 +558,27 @@
         return lax.ppermute(x, ("lat", "wall"), table)
 
     msg_rows = 2 * tiles * 5
-    moved, even_msg, odd_msg, vel_z, conc, flags, table = pl.pallas_call(
-        functools.partial(collide_kernel, chunks=chunks),
+    even_msg, odd_msg, pops, conc, flags, table = pl.pallas_call(
+        functools.partial(edges_kernel, chunks=chunks),
         out_shape=(
-            on_chip(DIRS, cells + 16, LANES),
             on_chip(msg_rows, LANES),
             on_chip(msg_rows, LANES),
-            on_chip(cells, LANES),
+            on_chip(DIRS + SPECIES, cells, LANES),
             on_chip(cells * SPECIES, LANES),
             on_chip(cells, LANES, dtype=jnp.int32),
-            on_chip(64, LANES),
+            on_chip(104, LANES),
         ),
         in_specs=[ANY_SPEC] * 6,
-        out_specs=(VMEM_SPEC,) * 7,
+        out_specs=(VMEM_SPEC,) * 6,
         scratch_shapes=[
-            pltpu.VMEM((DIRS + SPECIES, cells, LANES), F32),
-            pltpu.VMEM((10, cells, LANES), F32),
             pltpu.SMEM((SPECIES,), jnp.int32),
             pltpu.SMEM((SPECIES,), F32),
             pltpu.SMEM((3,), F32),
             pltpu.SemaphoreType.DMA((4 + len(chunks),)),
         ],
         compiler_params=params(),
-        cost_estimate=cost(5_000_000, 3_000_000),
-        name="collide",
+        cost_estimate=cost(2_000_000, 3_000_000),
+        name="edges",
     )(
         *in_hbm(
             populations.reshape(DIRS, cells, LANES),
@@ -594,15 +592,27 @@
     odd_got = move(odd_msg, odd)
     even_got = move(even_msg, even)
 
-    offset, edge, link, ends = pl.pallas_call(
+    mid, offset, edge, link, ends = pl.pallas_call(
         functools.partial(eliminate_kernel, rows=rows),
-        out_shape=(on_chip(cells * SPECIES, LANES),) * 3 + (on_chip(96, LANES),),
+        out_shape=(on_chip(10, cells, LANES),)
+        + (on_chip(cells * SPECIES, LANES),) * 3
+        + (on_chip(96, LANES),),
         in_specs=[VMEM_SPEC] * 4,
-        out_specs=(VMEM_SPEC,) * 4,
+        out_specs=(VMEM_SPEC,) * 5,
         compiler_params=params(),
         cost_estimate=cost(5_000_000, 3_000_000),
         name="eliminate",
-    )(*pin(vel_z, conc, flags, table))
+    )(*pin(pops, conc, flags, table))
+
+    moved = pl.pallas_call(
+        functools.partial(collide_kernel, tiles=tiles),
+        out_shape=on_chip(DIRS, cells + 16, LANES),
+        in_specs=[VMEM_SPEC] * 3,
+        out_specs=VMEM_SPEC,
+        compiler_params=params(),
+        cost_estimate=cost(5_000_000, 3_000_000),
+        name="collide",
+    )(*pin(pops, flags, mid))
 
     depth = len(levels)
     owns, gots = [ends], [move(ends, levels[0])]
@@ -611,18 +621,18 @@
         sent = pl.pallas_call(
             functools.partial(relay_kernel, level=level, last=last),
             out_shape=on_chip(32 if last else 96, LANES),
-            in_specs=[VMEM_SPEC] * 2,
+            in_specs=[VMEM_SPEC] * 3,
             out_specs=VMEM_SPEC,
             compiler_params=params(),
             cost_estimate=cost(100_000, 200_000),
             name=f"relay{level}",
-        )(*pin(owns[-1], gots[-1]))
+        )(*pin(owns[-1], gots[-1], moved))
         owns.append(sent)
         gots.append(move(sent, levels[level + 1]))
 
     faces = pl.pallas_call(
         functools.partial(faces_kernel, tiles=tiles),
-        out_shape=(on_chip(FACE_ROWS, LANES),) * depth,
+        out_shape=(on_chip(FACE_ROWS, LANES),) + (on_chip(FACE_ROWS + 8, LANES),) * (depth - 1),
         in_specs=[VMEM_SPEC] * 3,
         out_specs=(VMEM_SPEC,) * depth,
         compiler_params=params(),
@@ -659,7 +669,7 @@
         input_output_aliases={depth + 1: 0},
         scratch_shapes=[
             pltpu.VMEM((80, LANES), F32),
-            pltpu.SemaphoreType.DMA((10,)),
+            pltpu.SemaphoreType.DMA,
         ],
         compiler_params=params(),
         cost_estimate=cost(10_000, 100_000),

time: 13.9 us -> 13.6 us (0.978)
  waiting for transfers between devices: 1.37 us -> 1.03 us
  Pallas kernels: 4.26 us -> 4.48 us
  starting transfers between devices: 7.49 us -> 7.3 us
    ppermute x6, waiting for transfers between devices: 1.37 us -> 1.03 us  [move(): return lax.ppermute(x, ('lat', 'wall'), table)]
    pallas_call x1, Pallas kernels: 0.32 us -> 0.54 us  [per_device(): pl.pallas_call(functools.partial(eliminate_kernel, rows=rows), out_shape=...]
    ppermute x6, starting transfers between devices: 7.49 us -> 7.3 us  [move(): return lax.ppermute(x, ('lat', 'wall'), table)]
    pallas_call x1 -> x2, Pallas kernels: 1.88 us -> 1.97 us  [the longest x1 1.61 us: per_device(): pl.pallas_call(functools.partial(edges_kernel, chunks=chunks), out_shape=...]
  transfers between devices with their start and end apart: 6 -> 6, of which waited for: 3 -> 2; matrix products, arithmetic and copies ran while one was open for 0% -> 0% of each run, Pallas kernels for 12% -> 16%
where the time goes in v3:
time: 13.6 us; the launch traced here: 13.5 us
  starting transfers between devices  7.3 us (54%)
  Pallas kernels  4.48 us (33%)
  waiting for transfers between devices  1.03 us (8%)
  between operations  0.68 us (5%)
    ppermute x6, starting transfers between devices, move(): return lax.ppermute(x, ('lat', 'wall'), table)  7.3 us
    pallas_call x1, Pallas kernels, per_device(): pl.pallas_call(functools.partial(edges_kernel, chunks=chunks), out_shape=...  1.61 us
    pallas_call x1, Pallas kernels, per_device(): pl.pallas_call(functools.partial(outputs_kernel, rows=rows, tiles=tiles,...  1.29 us
    ppermute x6, waiting for transfers between devices, move(): return lax.ppermute(x, ('lat', 'wall'), table)  1.03 us
    pallas_call x1, Pallas kernels, per_device(): pl.pallas_call(functools.partial(patch_kernel, tiles=tiles, levels=depth)...  0.64 us
    pallas_call x1, Pallas kernels, per_device(): pl.pallas_call(functools.partial(eliminate_kernel, rows=rows), out_shape=...  0.54 us
    pallas_call x1, Pallas kernels, per_device(): pl.pallas_call(functools.partial(collide_kernel, tiles=tiles), out_shape=...  0.35 us
  transfers between devices with their start and end apart: 6, of which 2 were waited for; matrix products, arithmetic and copies ran while one was open for 0% of the time, Pallas kernels for 16%

profile of v3, /device:TPU:9, one launch (start us, length us, event | category | flops | bytes accessed | tf_op | source)
XLA Modules:
  0.0 13.5 jit_solution(17458396218153428267)
XLA Ops:
  0.6 1.6 %edges.1 = (f32[160,128]{1,0:T(8,128)S(1)}, f32[160,128]{1,0:T(8,128)S(1)}, f32[23,128,128]{2,1,0:T(8,128)S(1)}, f32[512,128]{1,0:T(8,128)S(1)}, s32[128,128]{1,0:T(8,128)S(1)}, /*index=5*/f32[104,128]{1,0:T(8,128)S(1)}) custom-call(f32[19,128,128]{2,1,0:T(8,128)} %bitcast.5, f32[512,128]{1,0:T(8,128)} %bitcast.7, s32[128,128]{1,0:T(8,128)} %bitcast.8, ...), custom_call_target="tpu_custom_call" | custom-call | flops 2000000 | bytes 3000000 | tf_op jit(solution)/shard_map/edges/pallas_call | solution.py:561
  2.3 1.3 %collective-permute-start = (f32[160,128]{1,0:T(8,128)S(1)}, f32[160,128]{1,0:T(8,128)S(1)}, u32[]{:S(2)}, u32[]{:S(2)}) collective-permute-start(f32[160,128]{1,0:T(8,128)S(1)} %get-tuple-element.23), channel_id=1, source_target_pairs={{0,4},{1,5},{2,6},{3,7},{4,0},{5,1},{6,2},{7,3},{8,12},{9,13},{10,... | collective-permute-start | bytes 245768 | tf_op jit(solution)/shard_map/ppermute | solution.py:558
  3.6 0.0 collective-permute-start.1
  3.6 0.5 %eliminate.1 = (f32[10,128,128]{2,1,0:T(8,128)S(1)}, f32[512,128]{1,0:T(8,128)S(1)}, f32[512,128]{1,0:T(8,128)S(1)}, f32[512,128]{1,0:T(8,128)S(1)}, f32[96,128]{1,0:T(8,128)S(1)}) custom-call(f32[23,128,128]{2,1,0:T(8,128)S(1)} %get-tuple-element.18.pops, f32[512,128]{1,0:T(8,128)S(1)} %get-tuple-element.20.conc, s32[128,128]{1,0:T(8,128)S(1)} %get-tuple-element.19.flags, ...), custom_call_target="tpu_custom_call" | custom-call | flops 5000000 | bytes 3000000 | tf_op jit(solution)/shard_map/eliminate/pallas_call | solution.py:595
  4.1 1.0 %collective-permute-start.4 = (f32[96,128]{1,0:T(8,128)S(1)}, f32[96,128]{1,0:T(8,128)S(1)}, u32[]{:S(2)}, u32[]{:S(2)}) collective-permute-start(f32[96,128]{1,0:T(8,128)S(1)} %get-tuple-element.27.own.refs_0_), channel_id=1, source_target_pairs={{0,1},{1,0},{2,3},{3,2},{4,5},{5,4},{6,7},{7,6},{8,9},{9,8},{10,11... | collective-permute-start | bytes 147464 | tf_op jit(solution)/shard_map/ppermute | solution.py:558
  5.1 0.4 %collide.1.moved._.refs_7_ = f32[19,144,128]{2,1,0:T(8,128)S(1)} custom-call(f32[23,128,128]{2,1,0:T(8,128)S(1)} %get-tuple-element.18.pops, s32[128,128]{1,0:T(8,128)S(1)} %get-tuple-element.19.flags, f32[10,128,128]{2,1,0:T(8,128)S(1)} %get-tuple-element.22.mid), custom_call_target="tpu_custom_call" | custom-call | flops 5000000 | bytes 3000000 | tf_op jit(solution)/shard_map/collide/pallas_call | solution.py:607
  5.5 0.5 %collective-permute-done.4.got.refs_2_ = f32[96,128]{1,0:T(8,128)S(1)} collective-permute-done((f32[96,128]{1,0:T(8,128)S(1)}, f32[96,128]{1,0:T(8,128)S(1)}, u32[]{:S(2)}, u32[]{:S(2)}) %collective-permute-start.4) | collective-permute-done | bytes 49184 | tf_op jit(solution)/shard_map/ppermute | solution.py:558
  6.0 1.9 %collective-permute-start.5 = (f32[32,128]{1,0:T(8,128)S(1)}, f32[32,128]{1,0:T(8,128)S(1)}, u32[]{:S(2)}, u32[]{:S(2)}) collective-permute-start(f32[32,128]{1,0:T(8,128)S(1)} %relay0.1.refs_1_), channel_id=1, source_target_pairs={{0,3},{1,2},{2,1},{3,0},{4,7},{5,6},{6,5},{7,4},{8,11},{9,10},{10,... | collective-permute-start | bytes 49160 | tf_op jit(solution)/shard_map/ppermute | solution.py:558
  7.9 0.0 collective-permute-done.even_got.refs_8_
  7.9 0.0 collective-permute-done.1.odd_got.refs_9_
  8.0 3.1 %collective-permute-start.3 = (f32[32,128]{1,0:T(8,128)S(1)}, f32[32,128]{1,0:T(8,128)S(1)}, u32[]{:S(2)}, u32[]{:S(2)}) collective-permute-start(f32[32,128]{1,0:T(8,128)S(1)} %get-tuple-element.26.refs_10_), channel_id=1, source_target_pairs={{0,3},{1,2},{2,1},{3,0},{4,7},{5,6},{6,5},{7,4},{8,11},{9,10},{10,... | collective-permute-start | bytes 49160 | tf_op jit(solution)/shard_map/ppermute | solution.py:558
  11.0 0.0 collective-permute-start.2
  11.0 0.0 collective-permute-done.5.refs_3_
  11.0 1.3 %outputs.1 = (f32[19,128,128]{2,1,0:T(8,128)}, f32[512,128]{1,0:T(8,128)}, f32[80,128]{1,0:T(8,128)S(1)}) custom-call(f32[96,128]{1,0:T(8,128)S(1)} %get-tuple-element.27.own.refs_0_, f32[32,128]{1,0:T(8,128)S(1)} %relay0.1.refs_1_, f32[96,128]{1,0:T(8,128)S(1)} %collective-permute-done.4.got.refs_2_, f32[32,128]{1,0:T(8,128)S(1)} %collective-permute-done.5.refs_3_, ...), custom_call_target="tpu_custom_call" | custom-call | flops 1000000 | bytes 2500000 | tf_op jit(solution)/shard_map/outputs/pallas_call | solution.py:645
  12.3 0.0 collective-permute-done.2.refs_0_
  12.3 0.5 %collective-permute-done.3.refs_1_ = f32[32,128]{1,0:T(8,128)S(1)} collective-permute-done((f32[32,128]{1,0:T(8,128)S(1)}, f32[32,128]{1,0:T(8,128)S(1)}, u32[]{:S(2)}, u32[]{:S(2)}) %collective-permute-start.3) | collective-permute-done | bytes 16416 | tf_op jit(solution)/shard_map/ppermute | solution.py:558
  12.8 0.6 %patch.1 = f32[19,128,128]{2,1,0:T(8,128)} custom-call(f32[24,128]{1,0:T(8,128)S(1)} %collective-permute-done.2.refs_0_, f32[32,128]{1,0:T(8,128)S(1)} %collective-permute-done.3.refs_1_, f32[80,128]{1,0:T(8,128)S(1)} %get-tuple-element.31.refs_2_, f32[19,128,128]{2,1,0:T(8,128)} %get-tuple-element.32.refs_3_), custom_call_target="tpu_custom_call", output_to_operand_aliasing={{}: (3, {})} | custom-call | flops 10000 | bytes 100000 | tf_op jit(solution)/shard_map/patch/pallas_call | solution.py:664
  (2 shorter events, 0.0 us)
Async XLA Ops:
  2.3 5.7 %collective-permute-start = (f32[160,128]{1,0:T(8,128)S(1)}, f32[160,128]{1,0:T(8,128)S(1)}, u32[]{:S(2)}, u32[]{:S(2)}) collective-permute-start(f32[160,128]{1,0:T(8,128)S(1)} %get-tuple-element.23), channel_id=1, source_target_pairs={{0,4},{1,5},{2,6},{3,7},{4,0},{5,1},{6,2},{7,3},{8,12},{9,13},{10,... | collective-permute-start | bytes 245768 | tf_op jit(solution)/shard_map/ppermute | solution.py:558
  3.6 4.4 %collective-permute-start.1 = (f32[160,128]{1,0:T(8,128)S(1)}, f32[160,128]{1,0:T(8,128)S(1)}, u32[]{:S(2)}, u32[]{:S(2)}) collective-permute-start(f32[160,128]{1,0:T(8,128)S(1)} %get-tuple-element.24), channel_id=1, source_target_pairs={{0,1},{1,0},{2,3},{3,2},{4,8},{5,9},{6,10},{7,11},{8,4},{9,5},{10,... | collective-permute-start | bytes 245768 | tf_op jit(solution)/shard_map/ppermute | solution.py:558
  4.1 1.9 %collective-permute-start.4 = (f32[96,128]{1,0:T(8,128)S(1)}, f32[96,128]{1,0:T(8,128)S(1)}, u32[]{:S(2)}, u32[]{:S(2)}) collective-permute-start(f32[96,128]{1,0:T(8,128)S(1)} %get-tuple-element.27.own.refs_0_), channel_id=1, source_target_pairs={{0,1},{1,0},{2,3},{3,2},{4,5},{5,4},{6,7},{7,6},{8,9},{9,8},{10,11... | collective-permute-start | bytes 147464 | tf_op jit(solution)/shard_map/ppermute | solution.py:558
  6.0 5.0 %collective-permute-start.5 = (f32[32,128]{1,0:T(8,128)S(1)}, f32[32,128]{1,0:T(8,128)S(1)}, u32[]{:S(2)}, u32[]{:S(2)}) collective-permute-start(f32[32,128]{1,0:T(8,128)S(1)} %relay0.1.refs_1_), channel_id=1, source_target_pairs={{0,3},{1,2},{2,1},{3,0},{4,7},{5,6},{6,5},{7,4},{8,11},{9,10},{10,... | collective-permute-start | bytes 49160 | tf_op jit(solution)/shard_map/ppermute | solution.py:558
  8.0 4.9 %collective-permute-start.3 = (f32[32,128]{1,0:T(8,128)S(1)}, f32[32,128]{1,0:T(8,128)S(1)}, u32[]{:S(2)}, u32[]{:S(2)}) collective-permute-start(f32[32,128]{1,0:T(8,128)S(1)} %get-tuple-element.26.refs_10_), channel_id=1, source_target_pairs={{0,3},{1,2},{2,1},{3,0},{4,7},{5,6},{6,5},{7,4},{8,11},{9,10},{10,... | collective-permute-start | bytes 49160 | tf_op jit(solution)/shard_map/ppermute | solution.py:558
  11.0 1.3 %collective-permute-start.2 = (f32[24,128]{1,0:T(8,128)S(1)}, f32[24,128]{1,0:T(8,128)S(1)}, u32[]{:S(2)}, u32[]{:S(2)}) collective-permute-start(f32[24,128]{1,0:T(8,128)S(1)} %get-tuple-element.25), channel_id=1, source_target_pairs={{0,1},{1,0},{2,3},{3,2},{4,5},{5,4},{6,7},{7,6},{8,9},{9,8},{10,11... | collective-permute-start | bytes 36872 | tf_op jit(solution)/shard_map/ppermute | solution.py:558

commit v4 on v3

--- a/solution.py
+++ b/solution.py
@@ -154,8 +154,6 @@
             )
         )
     ]
-    for copy in small:
-        copy.start()
     arrived = {}
     at = 0
     for c, count in enumerate(chunks):
@@ -167,6 +165,9 @@
         both = pops.at[:, rows]
         arrived[at] = pltpu.make_async_copy(both, both, sem)
         at += count
+        if c == 0:
+            for copy in small:
+                copy.start()
     low = low_rows()
     for copy in small:
         copy.wait()
@@ -215,7 +216,19 @@
             odd_msg[at] = jnp.where(is_odd, plus, minus)
 
 
-def collide_kernel(pops, flags, mid, moved, *, tiles):
+def write_faces(target, start, moved, level, tiles):
+    def fill(dirs):
+        for j, q in enumerate(dirs):
+            rows = pl.ds(8 * tiles + 8, 4) if lattice_dirs[q][2] > 0 else pl.ds(4, 4)
+            target[pl.ds(start + 4 * j, 4)] = moved[q, rows]
+        target[pl.ds(start + 20, 4)] = jnp.zeros((4, LANES), F32)
+
+    is_upper = bit(lax.axis_index("wall"), level) == 1
+    pl.when(jnp.logical_not(is_upper))(functools.partial(fill, z_plus))
+    pl.when(is_upper)(functools.partial(fill, z_minus))
+
+
+def collide_kernel(pops, flags, mid, moved, pair_faces, *, tiles):
     def scatter(at):
         solid = flags[pl.ds(at, 8)] != 0
         base, *rest = [mid[j, pl.ds(at, 8)] for j in range(10)]
@@ -241,6 +254,7 @@
     for d in z_plus + z_minus:
         at = 8 if lattice_dirs[d][2] > 0 else 8 * tiles + 4
         moved[d, pl.ds(at, 4)] = jnp.zeros((4, LANES), F32)
+    write_faces(pair_faces, 0, moved, 0, tiles)
 
 
 def reciprocal(x):
@@ -354,7 +368,7 @@
     return top_a, low_b, merged
 
 
-def relay_kernel(own, got, _, send, *, level, last):
+def relay_kernel(own, got, moved, send, *, level, last, tiles):
     wall = lax.axis_index("wall")
     is_upper = bit(wall, level) == 1
     next_upper = bit(wall, level + 1) == 1
@@ -368,9 +382,10 @@
             ]
         for j, value in enumerate(values):
             send[pl.ds(16 * j + 8 * h, 8)] = value
-
-
-def faces_kernel(moved, even_got, odd_got, *targets, tiles):
+    write_faces(send, 16 * len(values), moved, level + 1, tiles)
+
+
+def faces_kernel(even_got, odd_got, *targets, tiles):
     wall, lat = lax.axis_index("wall"), lax.axis_index("lat")
     lats = lax.axis_size("lat")
     odd_lat = lax.rem(lat, 2) == 1
@@ -384,14 +399,10 @@
         return jnp.where(exists, row, 0.0)
 
     def fill(target, dirs):
-        for j, q in enumerate(dirs):
+        target[...] = jnp.zeros(target.shape, F32)
+        for j, q in enumerate([q for q in dirs if lattice_dirs[q][0]]):
             up = lattice_dirs[q][2] > 0
-            target[pl.ds(4 * j, 4)] = moved[q, pl.ds(8 * tiles + 8, 4) if up else pl.ds(4, 4)]
-            step_x = lattice_dirs[q][0]
-            if step_x:
-                at = 4 * j + (0 if step_x > 0 else 3)
-                target[pl.ds(at, 1)] = from_lat(q, up, tiles - 1 if up else 0)
-        target[pl.ds(20, 4)] = jnp.zeros((4, LANES), F32)
+            target[pl.ds(j, 1)] = from_lat(q, up, tiles - 1 if up else 0)
 
     for r, target in enumerate(targets):
         pl.when(bit(wall, r) == 0)(functools.partial(fill, target, z_plus))
@@ -500,21 +511,28 @@
 
 
 def patch_kernel(*refs, tiles, levels):
-    gots = refs[:levels]
-    tops, _, pops_out, fixed, sem = refs[levels:]
+    gots, faces = refs[:levels], refs[levels : 2 * levels]
+    tops, _, pops_out, fixed, sem = refs[2 * levels :]
     wall = lax.axis_index("wall")
     for j in range(len(z_plus) + len(z_minus)):
         fixed[pl.ds(8 * j, 8)] = tops[pl.ds(8 * j, 8)]
 
-    def put(got, lower):
-        for j in range(5):
+    def put(r, lower):
+        base = 0 if r == 0 else 32 if r == levels - 1 else 96
+        row_of_x = 0
+        for j, q in enumerate(z_plus if lower else z_minus):
             row = 8 * j if lower else 8 * (5 + j) + 4
-            fixed[pl.ds(row, 4)] = got[pl.ds(4 * j, 4)]
+            fixed[pl.ds(row, 4)] = faces[r][pl.ds(base + 4 * j, 4)]
+            step_x = lattice_dirs[q][0]
+            if step_x:
+                row += 0 if step_x > 0 else 3
+                fixed[pl.ds(row, 1)] = gots[r][pl.ds(row_of_x, 1)]
+                row_of_x += 1
 
     for r in range(levels):
         rest = lax.rem(wall, 2 ** (r + 1))
-        pl.when(rest == 2**r)(functools.partial(put, gots[r], True))
-        pl.when(rest == 2**r - 1)(functools.partial(put, gots[r], False))
+        pl.when(rest == 2**r)(functools.partial(put, r, True))
+        pl.when(rest == 2**r - 1)(functools.partial(put, r, False))
     for j, q in enumerate(z_plus + z_minus):
         at = pl.ds(0, 8) if lattice_dirs[q][2] > 0 else pl.ds(8 * tiles - 8, 8)
         pltpu.make_async_copy(fixed.at[pl.ds(8 * j, 8)], pops_out.at[q, at], sem).start()
@@ -604,23 +622,24 @@
         name="eliminate",
     )(*pin(pops, conc, flags, table))
 
-    moved = pl.pallas_call(
+    moved, pair_faces = pl.pallas_call(
         functools.partial(collide_kernel, tiles=tiles),
-        out_shape=on_chip(DIRS, cells + 16, LANES),
+        out_shape=(on_chip(DIRS, cells + 16, LANES), on_chip(FACE_ROWS, LANES)),
         in_specs=[VMEM_SPEC] * 3,
-        out_specs=VMEM_SPEC,
+        out_specs=(VMEM_SPEC,) * 2,
         compiler_params=params(),
         cost_estimate=cost(5_000_000, 3_000_000),
         name="collide",
     )(*pin(pops, flags, mid))
 
     depth = len(levels)
+    pair_got = move(pair_faces, levels[0])
     owns, gots = [ends], [move(ends, levels[0])]
     for level in range(depth - 1):
         last = level == depth - 2
         sent = pl.pallas_call(
-            functools.partial(relay_kernel, level=level, last=last),
-            out_shape=on_chip(32 if last else 96, LANES),
+            functools.partial(relay_kernel, level=level, last=last, tiles=tiles),
+            out_shape=on_chip((32 if last else 96) + FACE_ROWS, LANES),
             in_specs=[VMEM_SPEC] * 3,
             out_specs=VMEM_SPEC,
             compiler_params=params(),
@@ -632,13 +651,13 @@
 
     faces = pl.pallas_call(
         functools.partial(faces_kernel, tiles=tiles),
-        out_shape=(on_chip(FACE_ROWS, LANES),) + (on_chip(FACE_ROWS + 8, LANES),) * (depth - 1),
-        in_specs=[VMEM_SPEC] * 3,
+        out_shape=(on_chip(8, LANES),) + (on_chip(16, LANES),) * (depth - 1),
+        in_specs=[VMEM_SPEC] * 2,
         out_specs=(VMEM_SPEC,) * depth,
         compiler_params=params(),
         cost_estimate=cost(100_000, 200_000),
         name="faces",
-    )(*pin(moved, even_got, odd_got))
+    )(*pin(even_got, odd_got))
     face_gots = [move(face, table) for face, table in zip(faces, levels)]
 
     operands = pin(*owns, *gots, offset, edge, link, moved, even_got, odd_got, faces[-1])
@@ -664,9 +683,9 @@
     new_pops = pl.pallas_call(
         functools.partial(patch_kernel, tiles=tiles, levels=depth),
         out_shape=jax.ShapeDtypeStruct((DIRS, cells, LANES), F32),
-        in_specs=[VMEM_SPEC] * (depth + 1) + [ANY_SPEC],
+        in_specs=[VMEM_SPEC] * (2 * depth + 1) + [ANY_SPEC],
         out_specs=ANY_SPEC,
-        input_output_aliases={depth + 1: 0},
+        input_output_aliases={2 * depth + 1: 0},
         scratch_shapes=[
             pltpu.VMEM((80, LANES), F32),
             pltpu.SemaphoreType.DMA,
@@ -674,7 +693,7 @@
         compiler_params=params(),
         cost_estimate=cost(10_000, 100_000),
         name="patch",
-    )(*pin(*face_gots, tops), pops_out)
+    )(*pin(*face_gots, pair_got, *gots[1:], tops), pops_out)
     return new_pops.reshape(populations.shape), new_conc.reshape(concentration.shape)
 
 

time: 13.6 us -> 13.4 us (0.985)
  waiting for transfers between devices: 1.03 us -> 0.85 us
    ppermute x6 -> x7, waiting for transfers between devices: 1.03 us -> 0.85 us  [move(): return lax.ppermute(x, ('lat', 'wall'), table)]
    ppermute x6 -> x7, starting transfers between devices: 7.3 us -> 7.29 us  [move(): return lax.ppermute(x, ('lat', 'wall'), table)]
  transfers between devices with their start and end apart: 6 -> 7, of which waited for: 2 -> 2; matrix products, arithmetic and copies ran while one was open for 0% -> 0% of each run, Pallas kernels for 16% -> 17%
where the time goes in v4:
time: 13.4 us; the launch traced here: 13.3 us
  starting transfers between devices  7.29 us (54%)
  Pallas kernels  4.48 us (33%)
  waiting for transfers between devices  0.85 us (6%)
  between operations  0.69 us (5%)
    ppermute x7, starting transfers between devices, move(): return lax.ppermute(x, ('lat', 'wall'), table)  7.29 us
    pallas_call x1, Pallas kernels, per_device(): pl.pallas_call(functools.partial(edges_kernel, chunks=chunks), out_shape=...  1.61 us
    pallas_call x1, Pallas kernels, per_device(): pl.pallas_call(functools.partial(outputs_kernel, rows=rows, tiles=tiles,...  1.29 us
    ppermute x7, waiting for transfers between devices, move(): return lax.ppermute(x, ('lat', 'wall'), table)  0.85 us
    pallas_call x1, Pallas kernels, per_device(): pl.pallas_call(functools.partial(patch_kernel, tiles=tiles, levels=depth)...  0.64 us
    pallas_call x1, Pallas kernels, per_device(): pl.pallas_call(functools.partial(eliminate_kernel, rows=rows), out_shape=...  0.55 us
    pallas_call x1, Pallas kernels, per_device(): pl.pallas_call(functools.partial(collide_kernel, tiles=tiles), out_shape=...  0.35 us
  transfers between devices with their start and end apart: 7, of which 2 were waited for; matrix products, arithmetic and copies ran while one was open for 0% of the time, Pallas kernels for 17%

profile of v4, /device:TPU:9, one launch (start us, length us, event | category | flops | bytes accessed | tf_op | source)
XLA Modules:
  0.0 13.3 jit_solution(3235251818597271854)
XLA Ops:
  0.6 1.6 %edges.1 = (f32[160,128]{1,0:T(8,128)S(1)}, f32[160,128]{1,0:T(8,128)S(1)}, f32[23,128,128]{2,1,0:T(8,128)S(1)}, f32[512,128]{1,0:T(8,128)S(1)}, s32[128,128]{1,0:T(8,128)S(1)}, /*index=5*/f32[104,128]{1,0:T(8,128)S(1)}) custom-call(f32[19,128,128]{2,1,0:T(8,128)} %bitcast.6, f32[512,128]{1,0:T(8,128)} %bitcast.7, s32[128,128]{1,0:T(8,128)} %bitcast.8, ...), custom_call_target="tpu_custom_call" | custom-call | flops 2000000 | bytes 3000000 | tf_op jit(solution)/shard_map/edges/pallas_call | solution.py:579
  2.2 1.3 %collective-permute-start = (f32[160,128]{1,0:T(8,128)S(1)}, f32[160,128]{1,0:T(8,128)S(1)}, u32[]{:S(2)}, u32[]{:S(2)}) collective-permute-start(f32[160,128]{1,0:T(8,128)S(1)} %get-tuple-element.20), channel_id=1, source_target_pairs={{0,4},{1,5},{2,6},{3,7},{4,0},{5,1},{6,2},{7,3},{8,12},{9,13},{10,... | collective-permute-start | bytes 245768 | tf_op jit(solution)/shard_map/ppermute | solution.py:576
  3.6 0.0 collective-permute-start.1
  3.6 0.5 %eliminate.1 = (f32[10,128,128]{2,1,0:T(8,128)S(1)}, f32[512,128]{1,0:T(8,128)S(1)}, f32[512,128]{1,0:T(8,128)S(1)}, f32[512,128]{1,0:T(8,128)S(1)}, f32[96,128]{1,0:T(8,128)S(1)}) custom-call(f32[23,128,128]{2,1,0:T(8,128)S(1)} %get-tuple-element.24.pops, f32[512,128]{1,0:T(8,128)S(1)} %get-tuple-element.26.conc, s32[128,128]{1,0:T(8,128)S(1)} %get-tuple-element.25.flags, ...), custom_call_target="tpu_custom_call" | custom-call | flops 5000000 | bytes 3000000 | tf_op jit(solution)/shard_map/eliminate/pallas_call | solution.py:613
  4.1 1.0 %collective-permute-start.5 = (f32[96,128]{1,0:T(8,128)S(1)}, f32[96,128]{1,0:T(8,128)S(1)}, u32[]{:S(2)}, u32[]{:S(2)}) collective-permute-start(f32[96,128]{1,0:T(8,128)S(1)} %get-tuple-element.30.own.refs_0_), channel_id=1, source_target_pairs={{0,1},{1,0},{2,3},{3,2},{4,5},{5,4},{6,7},{7,6},{8,9},{9,8},{10,11... | collective-permute-start | bytes 147464 | tf_op jit(solution)/shard_map/ppermute | solution.py:576
  5.1 0.4 %collide.1 = (f32[19,144,128]{2,1,0:T(8,128)S(1)}, f32[24,128]{1,0:T(8,128)S(1)}) custom-call(f32[23,128,128]{2,1,0:T(8,128)S(1)} %get-tuple-element.24.pops, s32[128,128]{1,0:T(8,128)S(1)} %get-tuple-element.25.flags, f32[10,128,128]{2,1,0:T(8,128)S(1)} %get-tuple-element.28.mid), custom_call_target="tpu_custom_call" | custom-call | flops 5000000 | bytes 3000000 | tf_op jit(solution)/shard_map/collide/pallas_call | solution.py:625
  5.5 0.5 %collective-permute-done.5.got.refs_2_ = f32[96,128]{1,0:T(8,128)S(1)} collective-permute-done((f32[96,128]{1,0:T(8,128)S(1)}, f32[96,128]{1,0:T(8,128)S(1)}, u32[]{:S(2)}, u32[]{:S(2)}) %collective-permute-start.5) | collective-permute-done | bytes 49184 | tf_op jit(solution)/shard_map/ppermute | solution.py:576
  6.0 1.9 %collective-permute-start.6 = (f32[56,128]{1,0:T(8,128)S(1)}, f32[56,128]{1,0:T(8,128)S(1)}, u32[]{:S(2)}, u32[]{:S(2)}) collective-permute-start(f32[56,128]{1,0:T(8,128)S(1)} %relay0.1.refs_1_), channel_id=1, source_target_pairs={{0,3},{1,2},{2,1},{3,0},{4,7},{5,6},{6,5},{7,4},{8,11},{9,10},{10,... | collective-permute-start | bytes 86024 | tf_op jit(solution)/shard_map/ppermute | solution.py:576
  7.9 0.2 %collective-permute-start.4 = (f32[24,128]{1,0:T(8,128)S(1)}, f32[24,128]{1,0:T(8,128)S(1)}, u32[]{:S(2)}, u32[]{:S(2)}) collective-permute-start(f32[24,128]{1,0:T(8,128)S(1)} %get-tuple-element.29), channel_id=1, source_target_pairs={{0,1},{1,0},{2,3},{3,2},{4,5},{5,4},{6,7},{7,6},{8,9},{9,8},{10,11... | collective-permute-start | bytes 36872 | tf_op jit(solution)/shard_map/ppermute | solution.py:576
  8.1 0.0 collective-permute-done.even_got.refs_8_
  8.1 0.0 collective-permute-done.1.odd_got.refs_9_
  8.1 2.9 %collective-permute-start.3 = (f32[16,128]{1,0:T(8,128)S(1)}, f32[16,128]{1,0:T(8,128)S(1)}, u32[]{:S(2)}, u32[]{:S(2)}) collective-permute-start(f32[16,128]{1,0:T(8,128)S(1)} %get-tuple-element.23.refs_10_), channel_id=1, source_target_pairs={{0,3},{1,2},{2,1},{3,0},{4,7},{5,6},{6,5},{7,4},{8,11},{9,10},{10,... | collective-permute-start | bytes 24584 | tf_op jit(solution)/shard_map/ppermute | solution.py:576
  11.0 0.0 collective-permute-start.2
  11.0 0.0 collective-permute-done.6.refs_3_
  11.0 1.3 %outputs.1 = (f32[19,128,128]{2,1,0:T(8,128)}, f32[512,128]{1,0:T(8,128)}, f32[80,128]{1,0:T(8,128)S(1)}) custom-call(f32[96,128]{1,0:T(8,128)S(1)} %get-tuple-element.30.own.refs_0_, f32[56,128]{1,0:T(8,128)S(1)} %relay0.1.refs_1_, f32[96,128]{1,0:T(8,128)S(1)} %collective-permute-done.5.got.refs_2_, f32[56,128]{1,0:T(8,128)S(1)} %collective-permute-done.6.refs_3_, ...), custom_call_target="tpu_custom_call" | custom-call | flops 1000000 | bytes 2500000 | tf_op jit(solution)/shard_map/outputs/pallas_call | solution.py:664
  12.3 0.0 collective-permute-done.4.refs_2_
  12.3 0.0 collective-permute-done.2.refs_0_
  12.4 0.3 %collective-permute-done.3.refs_1_ = f32[16,128]{1,0:T(8,128)S(1)} collective-permute-done((f32[16,128]{1,0:T(8,128)S(1)}, f32[16,128]{1,0:T(8,128)S(1)}, u32[]{:S(2)}, u32[]{:S(2)}) %collective-permute-start.3) | collective-permute-done | bytes 8224 | tf_op jit(solution)/shard_map/ppermute | solution.py:576
  12.7 0.6 %patch.1 = f32[19,128,128]{2,1,0:T(8,128)} custom-call(f32[8,128]{1,0:T(8,128)S(1)} %collective-permute-done.2.refs_0_, f32[16,128]{1,0:T(8,128)S(1)} %collective-permute-done.3.refs_1_, f32[24,128]{1,0:T(8,128)S(1)} %collective-permute-done.4.refs_2_, f32[56,128]{1,0:T(8,128)S(1)} %collective-permute-done.6.refs_3_, ...), custom_call_target="tpu_custom_call", output_to_operand_aliasing={{}: (5, {})} | custom-call | flops 10000 | bytes 100000 | tf_op jit(solution)/shard_map/patch/pallas_call | solution.py:683
  (2 shorter events, 0.0 us)
Async XLA Ops:
  2.2 5.9 %collective-permute-start = (f32[160,128]{1,0:T(8,128)S(1)}, f32[160,128]{1,0:T(8,128)S(1)}, u32[]{:S(2)}, u32[]{:S(2)}) collective-permute-start(f32[160,128]{1,0:T(8,128)S(1)} %get-tuple-element.20), channel_id=1, source_target_pairs={{0,4},{1,5},{2,6},{3,7},{4,0},{5,1},{6,2},{7,3},{8,12},{9,13},{10,... | collective-permute-start | bytes 245768 | tf_op jit(solution)/shard_map/ppermute | solution.py:576
  3.6 4.5 %collective-permute-start.1 = (f32[160,128]{1,0:T(8,128)S(1)}, f32[160,128]{1,0:T(8,128)S(1)}, u32[]{:S(2)}, u32[]{:S(2)}) collective-permute-start(f32[160,128]{1,0:T(8,128)S(1)} %get-tuple-element.21), channel_id=1, source_target_pairs={{0,1},{1,0},{2,3},{3,2},{4,8},{5,9},{6,10},{7,11},{8,4},{9,5},{10,... | collective-permute-start | bytes 245768 | tf_op jit(solution)/shard_map/ppermute | solution.py:576
  4.1 1.9 %collective-permute-start.5 = (f32[96,128]{1,0:T(8,128)S(1)}, f32[96,128]{1,0:T(8,128)S(1)}, u32[]{:S(2)}, u32[]{:S(2)}) collective-permute-start(f32[96,128]{1,0:T(8,128)S(1)} %get-tuple-element.30.own.refs_0_), channel_id=1, source_target_pairs={{0,1},{1,0},{2,3},{3,2},{4,5},{5,4},{6,7},{7,6},{8,9},{9,8},{10,11... | collective-permute-start | bytes 147464 | tf_op jit(solution)/shard_map/ppermute | solution.py:576
  6.0 5.0 %collective-permute-start.6 = (f32[56,128]{1,0:T(8,128)S(1)}, f32[56,128]{1,0:T(8,128)S(1)}, u32[]{:S(2)}, u32[]{:S(2)}) collective-permute-start(f32[56,128]{1,0:T(8,128)S(1)} %relay0.1.refs_1_), channel_id=1, source_target_pairs={{0,3},{1,2},{2,1},{3,0},{4,7},{5,6},{6,5},{7,4},{8,11},{9,10},{10,... | collective-permute-start | bytes 86024 | tf_op jit(solution)/shard_map/ppermute | solution.py:576
  7.9 4.4 %collective-permute-start.4 = (f32[24,128]{1,0:T(8,128)S(1)}, f32[24,128]{1,0:T(8,128)S(1)}, u32[]{:S(2)}, u32[]{:S(2)}) collective-permute-start(f32[24,128]{1,0:T(8,128)S(1)} %get-tuple-element.29), channel_id=1, source_target_pairs={{0,1},{1,0},{2,3},{3,2},{4,5},{5,4},{6,7},{7,6},{8,9},{9,8},{10,11... | collective-permute-start | bytes 36872 | tf_op jit(solution)/shard_map/ppermute | solution.py:576
  8.1 4.5 %collective-permute-start.3 = (f32[16,128]{1,0:T(8,128)S(1)}, f32[16,128]{1,0:T(8,128)S(1)}, u32[]{:S(2)}, u32[]{:S(2)}) collective-permute-start(f32[16,128]{1,0:T(8,128)S(1)} %get-tuple-element.23.refs_10_), channel_id=1, source_target_pairs={{0,3},{1,2},{2,1},{3,0},{4,7},{5,6},{6,5},{7,4},{8,11},{9,10},{10,... | collective-permute-start | bytes 24584 | tf_op jit(solution)/shard_map/ppermute | solution.py:576
  11.0 1.3 %collective-permute-start.2 = (f32[8,128]{1,0:T(8,128)S(1)}, f32[8,128]{1,0:T(8,128)S(1)}, u32[]{:S(2)}, u32[]{:S(2)}) collective-permute-start(f32[8,128]{1,0:T(8,128)S(1)} %get-tuple-element.22), channel_id=1, source_target_pairs={{0,1},{1,0},{2,3},{3,2},{4,5},{5,4},{6,7},{7,6},{8,9},{9,8},{10,11... | collective-permute-start | bytes 12296 | tf_op jit(solution)/shard_map/ppermute | solution.py:576

commit v5 on v4

--- a/solution.py
+++ b/solution.py
@@ -465,15 +465,13 @@
     lat, lats = lax.axis_index("lat"), lax.axis_size("lat")
     odd_lat = lax.rem(lat, 2) == 1
     body = pl.ds(8, 8 * tiles)
-    copies = []
-
-    def start(source, target):
-        copies.append(pltpu.make_async_copy(source, target, sems.at[len(copies)]))
-        copies[-1].start()
+
+    def start(source, target, sem):
+        pltpu.make_async_copy(source, target, sems.at[sem]).start()
 
     for q in range(DIRS):
         if lattice_dirs[q][0] == 0:
-            start(moved.at[q, body], pops_out.at[q])
+            start(moved.at[q, body], pops_out.at[q], 0)
     order = {q: j for j, q in enumerate(x_plus + x_minus)}
 
     def fill(dirs, got, keep):
@@ -496,18 +494,18 @@
         fill(x_minus, even_got, lat < lats - 1)
 
     for q in x_plus + x_minus:
-        start(patched.at[order[q], body], pops_out.at[q])
+        start(patched.at[order[q], body], pops_out.at[q], 0)
     for j, q in enumerate(z_plus + z_minus):
         at = pl.ds(8, 8) if lattice_dirs[q][2] > 0 else pl.ds(8 * tiles, 8)
         tops[pl.ds(8 * j, 8)] = patched[order[q], at] if q in order else moved[q, at]
 
     def write(_, begin, count):
         span = pl.ds(16 * begin, 16 * count)
-        start(solved.at[span], conc_out.at[span])
+        start(solved.at[span], conc_out.at[span], 1)
 
     solve_ions(owns, gots, offset, edge, link, solved, write, rows=rows)
-    for copy in copies:
-        copy.wait()
+    pltpu.make_async_copy(pops_out, pops_out, sems.at[0]).wait()
+    pltpu.make_async_copy(solved, solved, sems.at[1]).wait()
 
 
 def patch_kernel(*refs, tiles, levels):
@@ -673,7 +671,7 @@
         scratch_shapes=[
             pltpu.VMEM((10, cells + 16, LANES), F32),
             pltpu.VMEM((cells * SPECIES, LANES), F32),
-            pltpu.SemaphoreType.DMA((DIRS + 3,)),
+            pltpu.SemaphoreType.DMA((2,)),
         ],
         compiler_params=params(),
         cost_estimate=cost(1_000_000, 2_500_000),

time: 13.4 us -> 13.4 us (level)
  waiting for transfers between devices: 0.85 us -> 1.04 us
  Pallas kernels: 4.48 us -> 4.3 us
    ppermute x7, waiting for transfers between devices: 0.85 us -> 1.04 us  [move(): return lax.ppermute(x, ('lat', 'wall'), table)]
    pallas_call x1, Pallas kernels: 1.29 us -> 1.11 us  [per_device(): pl.pallas_call(functools.partial(outputs_kernel, rows=rows, tiles=tiles,...]
  transfers between devices with their start and end apart: 7 -> 7, of which waited for: 2 -> 2; matrix products, arithmetic and copies ran while one was open for 0% -> 0% of each run, Pallas kernels for 17% -> 15%
where the time goes in v5:
time: 13.4 us; the launch traced here: 13.3 us
  starting transfers between devices  7.29 us (54%)
  Pallas kernels  4.3 us (32%)
  waiting for transfers between devices  1.04 us (8%)
  between operations  0.68 us (5%)
    ppermute x7, starting transfers between devices, move(): return lax.ppermute(x, ('lat', 'wall'), table)  7.29 us
    pallas_call x1, Pallas kernels, per_device(): pl.pallas_call(functools.partial(edges_kernel, chunks=chunks), out_shape=...  1.61 us
    pallas_call x1, Pallas kernels, per_device(): pl.pallas_call(functools.partial(outputs_kernel, rows=rows, tiles=tiles,...  1.11 us
    ppermute x7, waiting for transfers between devices, move(): return lax.ppermute(x, ('lat', 'wall'), table)  1.04 us
    pallas_call x1, Pallas kernels, per_device(): pl.pallas_call(functools.partial(patch_kernel, tiles=tiles, levels=depth)...  0.64 us
    pallas_call x1, Pallas kernels, per_device(): pl.pallas_call(functools.partial(eliminate_kernel, rows=rows), out_shape=...  0.55 us
    pallas_call x1, Pallas kernels, per_device(): pl.pallas_call(functools.partial(collide_kernel, tiles=tiles), out_shape=...  0.35 us
  transfers between devices with their start and end apart: 7, of which 2 were waited for; matrix products, arithmetic and copies ran while one was open for 0% of the time, Pallas kernels for 15%

profile of v5, /device:TPU:9, one launch (start us, length us, event | category | flops | bytes accessed | tf_op | source)
XLA Modules:
  0.0 13.3 jit_solution(2551262553325543789)
XLA Ops:
  0.6 1.6 %edges.1 = (f32[160,128]{1,0:T(8,128)S(1)}, f32[160,128]{1,0:T(8,128)S(1)}, f32[23,128,128]{2,1,0:T(8,128)S(1)}, f32[512,128]{1,0:T(8,128)S(1)}, s32[128,128]{1,0:T(8,128)S(1)}, /*index=5*/f32[104,128]{1,0:T(8,128)S(1)}) custom-call(f32[19,128,128]{2,1,0:T(8,128)} %bitcast.6, f32[512,128]{1,0:T(8,128)} %bitcast.7, s32[128,128]{1,0:T(8,128)} %bitcast.8, ...), custom_call_target="tpu_custom_call" | custom-call | flops 2000000 | bytes 3000000 | tf_op jit(solution)/shard_map/edges/pallas_call | solution.py:577
  2.2 1.3 %collective-permute-start = (f32[160,128]{1,0:T(8,128)S(1)}, f32[160,128]{1,0:T(8,128)S(1)}, u32[]{:S(2)}, u32[]{:S(2)}) collective-permute-start(f32[160,128]{1,0:T(8,128)S(1)} %get-tuple-element.20), channel_id=1, source_target_pairs={{0,4},{1,5},{2,6},{3,7},{4,0},{5,1},{6,2},{7,3},{8,12},{9,13},{10,... | collective-permute-start | bytes 245768 | tf_op jit(solution)/shard_map/ppermute | solution.py:574
  3.6 0.0 collective-permute-start.1
  3.6 0.5 %eliminate.1 = (f32[10,128,128]{2,1,0:T(8,128)S(1)}, f32[512,128]{1,0:T(8,128)S(1)}, f32[512,128]{1,0:T(8,128)S(1)}, f32[512,128]{1,0:T(8,128)S(1)}, f32[96,128]{1,0:T(8,128)S(1)}) custom-call(f32[23,128,128]{2,1,0:T(8,128)S(1)} %get-tuple-element.24.pops, f32[512,128]{1,0:T(8,128)S(1)} %get-tuple-element.26.conc, s32[128,128]{1,0:T(8,128)S(1)} %get-tuple-element.25.flags, ...), custom_call_target="tpu_custom_call" | custom-call | flops 5000000 | bytes 3000000 | tf_op jit(solution)/shard_map/eliminate/pallas_call | solution.py:611
  4.1 1.0 %collective-permute-start.5 = (f32[96,128]{1,0:T(8,128)S(1)}, f32[96,128]{1,0:T(8,128)S(1)}, u32[]{:S(2)}, u32[]{:S(2)}) collective-permute-start(f32[96,128]{1,0:T(8,128)S(1)} %get-tuple-element.30.own.refs_0_), channel_id=1, source_target_pairs={{0,1},{1,0},{2,3},{3,2},{4,5},{5,4},{6,7},{7,6},{8,9},{9,8},{10,11... | collective-permute-start | bytes 147464 | tf_op jit(solution)/shard_map/ppermute | solution.py:574
  5.1 0.4 %collide.1 = (f32[19,144,128]{2,1,0:T(8,128)S(1)}, f32[24,128]{1,0:T(8,128)S(1)}) custom-call(f32[23,128,128]{2,1,0:T(8,128)S(1)} %get-tuple-element.24.pops, s32[128,128]{1,0:T(8,128)S(1)} %get-tuple-element.25.flags, f32[10,128,128]{2,1,0:T(8,128)S(1)} %get-tuple-element.28.mid), custom_call_target="tpu_custom_call" | custom-call | flops 5000000 | bytes 3000000 | tf_op jit(solution)/shard_map/collide/pallas_call | solution.py:623
  5.5 0.5 %collective-permute-done.5.got.refs_2_ = f32[96,128]{1,0:T(8,128)S(1)} collective-permute-done((f32[96,128]{1,0:T(8,128)S(1)}, f32[96,128]{1,0:T(8,128)S(1)}, u32[]{:S(2)}, u32[]{:S(2)}) %collective-permute-start.5) | collective-permute-done | bytes 49184 | tf_op jit(solution)/shard_map/ppermute | solution.py:574
  6.0 1.9 %collective-permute-start.6 = (f32[56,128]{1,0:T(8,128)S(1)}, f32[56,128]{1,0:T(8,128)S(1)}, u32[]{:S(2)}, u32[]{:S(2)}) collective-permute-start(f32[56,128]{1,0:T(8,128)S(1)} %relay0.1.refs_1_), channel_id=1, source_target_pairs={{0,3},{1,2},{2,1},{3,0},{4,7},{5,6},{6,5},{7,4},{8,11},{9,10},{10,... | collective-permute-start | bytes 86024 | tf_op jit(solution)/shard_map/ppermute | solution.py:574
  7.9 0.2 %collective-permute-start.4 = (f32[24,128]{1,0:T(8,128)S(1)}, f32[24,128]{1,0:T(8,128)S(1)}, u32[]{:S(2)}, u32[]{:S(2)}) collective-permute-start(f32[24,128]{1,0:T(8,128)S(1)} %get-tuple-element.29), channel_id=1, source_target_pairs={{0,1},{1,0},{2,3},{3,2},{4,5},{5,4},{6,7},{7,6},{8,9},{9,8},{10,11... | collective-permute-start | bytes 36872 | tf_op jit(solution)/shard_map/ppermute | solution.py:574
  8.1 0.0 collective-permute-done.even_got.refs_8_
  8.1 0.0 collective-permute-done.1.odd_got.refs_9_
  8.1 2.9 %collective-permute-start.3 = (f32[16,128]{1,0:T(8,128)S(1)}, f32[16,128]{1,0:T(8,128)S(1)}, u32[]{:S(2)}, u32[]{:S(2)}) collective-permute-start(f32[16,128]{1,0:T(8,128)S(1)} %get-tuple-element.23.refs_10_), channel_id=1, source_target_pairs={{0,3},{1,2},{2,1},{3,0},{4,7},{5,6},{6,5},{7,4},{8,11},{9,10},{10,... | collective-permute-start | bytes 24584 | tf_op jit(solution)/shard_map/ppermute | solution.py:574
  11.0 0.0 collective-permute-start.2
  11.0 0.0 collective-permute-done.6.refs_3_
  11.0 1.1 %outputs.1 = (f32[19,128,128]{2,1,0:T(8,128)}, f32[512,128]{1,0:T(8,128)}, f32[80,128]{1,0:T(8,128)S(1)}) custom-call(f32[96,128]{1,0:T(8,128)S(1)} %get-tuple-element.30.own.refs_0_, f32[56,128]{1,0:T(8,128)S(1)} %relay0.1.refs_1_, f32[96,128]{1,0:T(8,128)S(1)} %collective-permute-done.5.got.refs_2_, f32[56,128]{1,0:T(8,128)S(1)} %collective-permute-done.6.refs_3_, ...), custom_call_target="tpu_custom_call" | custom-call | flops 1000000 | bytes 2500000 | tf_op jit(solution)/shard_map/outputs/pallas_call | solution.py:662
  12.2 0.0 collective-permute-done.4.refs_2_
  12.2 0.0 collective-permute-done.2.refs_0_
  12.2 0.5 %collective-permute-done.3.refs_1_ = f32[16,128]{1,0:T(8,128)S(1)} collective-permute-done((f32[16,128]{1,0:T(8,128)S(1)}, f32[16,128]{1,0:T(8,128)S(1)}, u32[]{:S(2)}, u32[]{:S(2)}) %collective-permute-start.3) | collective-permute-done | bytes 8224 | tf_op jit(solution)/shard_map/ppermute | solution.py:574
  12.7 0.6 %patch.1 = f32[19,128,128]{2,1,0:T(8,128)} custom-call(f32[8,128]{1,0:T(8,128)S(1)} %collective-permute-done.2.refs_0_, f32[16,128]{1,0:T(8,128)S(1)} %collective-permute-done.3.refs_1_, f32[24,128]{1,0:T(8,128)S(1)} %collective-permute-done.4.refs_2_, f32[56,128]{1,0:T(8,128)S(1)} %collective-permute-done.6.refs_3_, ...), custom_call_target="tpu_custom_call", output_to_operand_aliasing={{}: (5, {})} | custom-call | flops 10000 | bytes 100000 | tf_op jit(solution)/shard_map/patch/pallas_call | solution.py:681
  (2 shorter events, 0.0 us)
Async XLA Ops:
  2.2 5.9 %collective-permute-start = (f32[160,128]{1,0:T(8,128)S(1)}, f32[160,128]{1,0:T(8,128)S(1)}, u32[]{:S(2)}, u32[]{:S(2)}) collective-permute-start(f32[160,128]{1,0:T(8,128)S(1)} %get-tuple-element.20), channel_id=1, source_target_pairs={{0,4},{1,5},{2,6},{3,7},{4,0},{5,1},{6,2},{7,3},{8,12},{9,13},{10,... | collective-permute-start | bytes 245768 | tf_op jit(solution)/shard_map/ppermute | solution.py:574
  3.6 4.5 %collective-permute-start.1 = (f32[160,128]{1,0:T(8,128)S(1)}, f32[160,128]{1,0:T(8,128)S(1)}, u32[]{:S(2)}, u32[]{:S(2)}) collective-permute-start(f32[160,128]{1,0:T(8,128)S(1)} %get-tuple-element.21), channel_id=1, source_target_pairs={{0,1},{1,0},{2,3},{3,2},{4,8},{5,9},{6,10},{7,11},{8,4},{9,5},{10,... | collective-permute-start | bytes 245768 | tf_op jit(solution)/shard_map/ppermute | solution.py:574
  4.1 1.9 %collective-permute-start.5 = (f32[96,128]{1,0:T(8,128)S(1)}, f32[96,128]{1,0:T(8,128)S(1)}, u32[]{:S(2)}, u32[]{:S(2)}) collective-permute-start(f32[96,128]{1,0:T(8,128)S(1)} %get-tuple-element.30.own.refs_0_), channel_id=1, source_target_pairs={{0,1},{1,0},{2,3},{3,2},{4,5},{5,4},{6,7},{7,6},{8,9},{9,8},{10,11... | collective-permute-start | bytes 147464 | tf_op jit(solution)/shard_map/ppermute | solution.py:574
  6.0 5.0 %collective-permute-start.6 = (f32[56,128]{1,0:T(8,128)S(1)}, f32[56,128]{1,0:T(8,128)S(1)}, u32[]{:S(2)}, u32[]{:S(2)}) collective-permute-start(f32[56,128]{1,0:T(8,128)S(1)} %relay0.1.refs_1_), channel_id=1, source_target_pairs={{0,3},{1,2},{2,1},{3,0},{4,7},{5,6},{6,5},{7,4},{8,11},{9,10},{10,... | collective-permute-start | bytes 86024 | tf_op jit(solution)/shard_map/ppermute | solution.py:574
  7.9 4.2 %collective-permute-start.4 = (f32[24,128]{1,0:T(8,128)S(1)}, f32[24,128]{1,0:T(8,128)S(1)}, u32[]{:S(2)}, u32[]{:S(2)}) collective-permute-start(f32[24,128]{1,0:T(8,128)S(1)} %get-tuple-element.29), channel_id=1, source_target_pairs={{0,1},{1,0},{2,3},{3,2},{4,5},{5,4},{6,7},{7,6},{8,9},{9,8},{10,11... | collective-permute-start | bytes 36872 | tf_op jit(solution)/shard_map/ppermute | solution.py:574
  8.1 4.5 %collective-permute-start.3 = (f32[16,128]{1,0:T(8,128)S(1)}, f32[16,128]{1,0:T(8,128)S(1)}, u32[]{:S(2)}, u32[]{:S(2)}) collective-permute-start(f32[16,128]{1,0:T(8,128)S(1)} %get-tuple-element.23.refs_10_), channel_id=1, source_target_pairs={{0,3},{1,2},{2,1},{3,0},{4,7},{5,6},{6,5},{7,4},{8,11},{9,10},{10,... | collective-permute-start | bytes 24584 | tf_op jit(solution)/shard_map/ppermute | solution.py:574
  11.0 1.2 %collective-permute-start.2 = (f32[8,128]{1,0:T(8,128)S(1)}, f32[8,128]{1,0:T(8,128)S(1)}, u32[]{:S(2)}, u32[]{:S(2)}) collective-permute-start(f32[8,128]{1,0:T(8,128)S(1)} %get-tuple-element.22), channel_id=1, source_target_pairs={{0,1},{1,0},{2,3},{3,2},{4,5},{5,4},{6,7},{7,6},{8,9},{9,8},{10,11... | collective-permute-start | bytes 12296 | tf_op jit(solution)/shard_map/ppermute | solution.py:574

commit v6 on v5

--- a/solution.py
+++ b/solution.py
@@ -649,7 +649,7 @@
 
     faces = pl.pallas_call(
         functools.partial(faces_kernel, tiles=tiles),
-        out_shape=(on_chip(8, LANES),) + (on_chip(16, LANES),) * (depth - 1),
+        out_shape=(on_chip(8, LANES),) + (on_chip(8, LANES),) * (depth - 1),
         in_specs=[VMEM_SPEC] * 2,
         out_specs=(VMEM_SPEC,) * depth,
         compiler_params=params(),

time: 13.4 us -> 13.4 us (level)
  no operation moved by 1% of the time
where the time goes in v6:
time: 13.4 us; the launch traced here: 13.2 us
  starting transfers between devices  7.3 us (54%)
  Pallas kernels  4.3 us (32%)
  waiting for transfers between devices  0.95 us (7%)
  between operations  0.68 us (5%)
    ppermute x7, starting transfers between devices, move(): return lax.ppermute(x, ('lat', 'wall'), table)  7.3 us
    pallas_call x1, Pallas kernels, per_device(): pl.pallas_call(functools.partial(edges_kernel, chunks=chunks), out_shape=...  1.61 us
    pallas_call x1, Pallas kernels, per_device(): pl.pallas_call(functools.partial(outputs_kernel, rows=rows, tiles=tiles,...  1.11 us
    ppermute x7, waiting for transfers between devices, move(): return lax.ppermute(x, ('lat', 'wall'), table)  0.95 us
    pallas_call x1, Pallas kernels, per_device(): pl.pallas_call(functools.partial(patch_kernel, tiles=tiles, levels=depth)...  0.65 us
    pallas_call x1, Pallas kernels, per_device(): pl.pallas_call(functools.partial(eliminate_kernel, rows=rows), out_shape=...  0.54 us
    pallas_call x1, Pallas kernels, per_device(): pl.pallas_call(functools.partial(collide_kernel, tiles=tiles), out_shape=...  0.35 us
  transfers between devices with their start and end apart: 7, of which 2 were waited for; matrix products, arithmetic and copies ran while one was open for 0% of the time, Pallas kernels for 15%

profile of v6, /device:TPU:9, one launch (start us, length us, event | category | flops | bytes accessed | tf_op | source)
XLA Modules:
  0.0 13.2 jit_solution(8114237291907255655)
XLA Ops:
  0.6 1.6 %edges.1 = (f32[160,128]{1,0:T(8,128)S(1)}, f32[160,128]{1,0:T(8,128)S(1)}, f32[23,128,128]{2,1,0:T(8,128)S(1)}, f32[512,128]{1,0:T(8,128)S(1)}, s32[128,128]{1,0:T(8,128)S(1)}, /*index=5*/f32[104,128]{1,0:T(8,128)S(1)}) custom-call(f32[19,128,128]{2,1,0:T(8,128)} %bitcast.6, f32[512,128]{1,0:T(8,128)} %bitcast.7, s32[128,128]{1,0:T(8,128)} %bitcast.8, ...), custom_call_target="tpu_custom_call" | custom-call | flops 2000000 | bytes 3000000 | tf_op jit(solution)/shard_map/edges/pallas_call | solution.py:577
  2.2 1.3 %collective-permute-start = (f32[160,128]{1,0:T(8,128)S(1)}, f32[160,128]{1,0:T(8,128)S(1)}, u32[]{:S(2)}, u32[]{:S(2)}) collective-permute-start(f32[160,128]{1,0:T(8,128)S(1)} %get-tuple-element.20), channel_id=1, source_target_pairs={{0,4},{1,5},{2,6},{3,7},{4,0},{5,1},{6,2},{7,3},{8,12},{9,13},{10,... | collective-permute-start | bytes 245768 | tf_op jit(solution)/shard_map/ppermute | solution.py:574
  3.6 0.0 collective-permute-start.1
  3.6 0.5 %eliminate.1 = (f32[10,128,128]{2,1,0:T(8,128)S(1)}, f32[512,128]{1,0:T(8,128)S(1)}, f32[512,128]{1,0:T(8,128)S(1)}, f32[512,128]{1,0:T(8,128)S(1)}, f32[96,128]{1,0:T(8,128)S(1)}) custom-call(f32[23,128,128]{2,1,0:T(8,128)S(1)} %get-tuple-element.24.pops, f32[512,128]{1,0:T(8,128)S(1)} %get-tuple-element.26.conc, s32[128,128]{1,0:T(8,128)S(1)} %get-tuple-element.25.flags, ...), custom_call_target="tpu_custom_call" | custom-call | flops 5000000 | bytes 3000000 | tf_op jit(solution)/shard_map/eliminate/pallas_call | solution.py:611
  4.1 1.0 %collective-permute-start.5 = (f32[96,128]{1,0:T(8,128)S(1)}, f32[96,128]{1,0:T(8,128)S(1)}, u32[]{:S(2)}, u32[]{:S(2)}) collective-permute-start(f32[96,128]{1,0:T(8,128)S(1)} %get-tuple-element.30.own.refs_0_), channel_id=1, source_target_pairs={{0,1},{1,0},{2,3},{3,2},{4,5},{5,4},{6,7},{7,6},{8,9},{9,8},{10,11... | collective-permute-start | bytes 147464 | tf_op jit(solution)/shard_map/ppermute | solution.py:574
  5.1 0.4 %collide.1 = (f32[19,144,128]{2,1,0:T(8,128)S(1)}, f32[24,128]{1,0:T(8,128)S(1)}) custom-call(f32[23,128,128]{2,1,0:T(8,128)S(1)} %get-tuple-element.24.pops, s32[128,128]{1,0:T(8,128)S(1)} %get-tuple-element.25.flags, f32[10,128,128]{2,1,0:T(8,128)S(1)} %get-tuple-element.28.mid), custom_call_target="tpu_custom_call" | custom-call | flops 5000000 | bytes 3000000 | tf_op jit(solution)/shard_map/collide/pallas_call | solution.py:623
  5.5 0.5 %collective-permute-done.5.got.refs_2_ = f32[96,128]{1,0:T(8,128)S(1)} collective-permute-done((f32[96,128]{1,0:T(8,128)S(1)}, f32[96,128]{1,0:T(8,128)S(1)}, u32[]{:S(2)}, u32[]{:S(2)}) %collective-permute-start.5) | collective-permute-done | bytes 49184 | tf_op jit(solution)/shard_map/ppermute | solution.py:574
  6.0 1.9 %collective-permute-start.6 = (f32[56,128]{1,0:T(8,128)S(1)}, f32[56,128]{1,0:T(8,128)S(1)}, u32[]{:S(2)}, u32[]{:S(2)}) collective-permute-start(f32[56,128]{1,0:T(8,128)S(1)} %relay0.1.refs_1_), channel_id=1, source_target_pairs={{0,3},{1,2},{2,1},{3,0},{4,7},{5,6},{6,5},{7,4},{8,11},{9,10},{10,... | collective-permute-start | bytes 86024 | tf_op jit(solution)/shard_map/ppermute | solution.py:574
  7.9 0.2 %collective-permute-start.4 = (f32[24,128]{1,0:T(8,128)S(1)}, f32[24,128]{1,0:T(8,128)S(1)}, u32[]{:S(2)}, u32[]{:S(2)}) collective-permute-start(f32[24,128]{1,0:T(8,128)S(1)} %get-tuple-element.29), channel_id=1, source_target_pairs={{0,1},{1,0},{2,3},{3,2},{4,5},{5,4},{6,7},{7,6},{8,9},{9,8},{10,11... | collective-permute-start | bytes 36872 | tf_op jit(solution)/shard_map/ppermute | solution.py:574
  8.1 0.0 collective-permute-done.even_got.refs_8_
  8.1 0.0 collective-permute-done.1.odd_got.refs_9_
  8.1 2.9 %collective-permute-start.3 = (f32[8,128]{1,0:T(8,128)S(1)}, f32[8,128]{1,0:T(8,128)S(1)}, u32[]{:S(2)}, u32[]{:S(2)}) collective-permute-start(f32[8,128]{1,0:T(8,128)S(1)} %get-tuple-element.23.refs_10_), channel_id=1, source_target_pairs={{0,3},{1,2},{2,1},{3,0},{4,7},{5,6},{6,5},{7,4},{8,11},{9,10},{10,... | collective-permute-start | bytes 12296 | tf_op jit(solution)/shard_map/ppermute | solution.py:574
  11.0 0.0 collective-permute-start.2
  11.0 0.0 collective-permute-done.6.refs_3_
  11.0 1.1 %outputs.1 = (f32[19,128,128]{2,1,0:T(8,128)}, f32[512,128]{1,0:T(8,128)}, f32[80,128]{1,0:T(8,128)S(1)}) custom-call(f32[96,128]{1,0:T(8,128)S(1)} %get-tuple-element.30.own.refs_0_, f32[56,128]{1,0:T(8,128)S(1)} %relay0.1.refs_1_, f32[96,128]{1,0:T(8,128)S(1)} %collective-permute-done.5.got.refs_2_, f32[56,128]{1,0:T(8,128)S(1)} %collective-permute-done.6.refs_3_, ...), custom_call_target="tpu_custom_call" | custom-call | flops 1000000 | bytes 2500000 | tf_op jit(solution)/shard_map/outputs/pallas_call | solution.py:662
  12.2 0.0 collective-permute-done.4.refs_2_
  12.2 0.4 %collective-permute-done.3.refs_1_ = f32[8,128]{1,0:T(8,128)S(1)} collective-permute-done((f32[8,128]{1,0:T(8,128)S(1)}, f32[8,128]{1,0:T(8,128)S(1)}, u32[]{:S(2)}, u32[]{:S(2)}) %collective-permute-start.3) | collective-permute-done | bytes 4128 | tf_op jit(solution)/shard_map/ppermute | solution.py:574
  12.6 0.0 collective-permute-done.2.refs_0_
  12.6 0.7 %patch.1 = f32[19,128,128]{2,1,0:T(8,128)} custom-call(f32[8,128]{1,0:T(8,128)S(1)} %collective-permute-done.2.refs_0_, f32[8,128]{1,0:T(8,128)S(1)} %collective-permute-done.3.refs_1_, f32[24,128]{1,0:T(8,128)S(1)} %collective-permute-done.4.refs_2_, f32[56,128]{1,0:T(8,128)S(1)} %collective-permute-done.6.refs_3_, ...), custom_call_target="tpu_custom_call", output_to_operand_aliasing={{}: (5, {})} | custom-call | flops 10000 | bytes 100000 | tf_op jit(solution)/shard_map/patch/pallas_call | solution.py:681
  (2 shorter events, 0.0 us)
Async XLA Ops:
  2.2 5.8 %collective-permute-start = (f32[160,128]{1,0:T(8,128)S(1)}, f32[160,128]{1,0:T(8,128)S(1)}, u32[]{:S(2)}, u32[]{:S(2)}) collective-permute-start(f32[160,128]{1,0:T(8,128)S(1)} %get-tuple-element.20), channel_id=1, source_target_pairs={{0,4},{1,5},{2,6},{3,7},{4,0},{5,1},{6,2},{7,3},{8,12},{9,13},{10,... | collective-permute-start | bytes 245768 | tf_op jit(solution)/shard_map/ppermute | solution.py:574
  3.6 4.5 %collective-permute-start.1 = (f32[160,128]{1,0:T(8,128)S(1)}, f32[160,128]{1,0:T(8,128)S(1)}, u32[]{:S(2)}, u32[]{:S(2)}) collective-permute-start(f32[160,128]{1,0:T(8,128)S(1)} %get-tuple-element.21), channel_id=1, source_target_pairs={{0,1},{1,0},{2,3},{3,2},{4,8},{5,9},{6,10},{7,11},{8,4},{9,5},{10,... | collective-permute-start | bytes 245768 | tf_op jit(solution)/shard_map/ppermute | solution.py:574
  4.1 1.9 %collective-permute-start.5 = (f32[96,128]{1,0:T(8,128)S(1)}, f32[96,128]{1,0:T(8,128)S(1)}, u32[]{:S(2)}, u32[]{:S(2)}) collective-permute-start(f32[96,128]{1,0:T(8,128)S(1)} %get-tuple-element.30.own.refs_0_), channel_id=1, source_target_pairs={{0,1},{1,0},{2,3},{3,2},{4,5},{5,4},{6,7},{7,6},{8,9},{9,8},{10,11... | collective-permute-start | bytes 147464 | tf_op jit(solution)/shard_map/ppermute | solution.py:574
  6.0 5.0 %collective-permute-start.6 = (f32[56,128]{1,0:T(8,128)S(1)}, f32[56,128]{1,0:T(8,128)S(1)}, u32[]{:S(2)}, u32[]{:S(2)}) collective-permute-start(f32[56,128]{1,0:T(8,128)S(1)} %relay0.1.refs_1_), channel_id=1, source_target_pairs={{0,3},{1,2},{2,1},{3,0},{4,7},{5,6},{6,5},{7,4},{8,11},{9,10},{10,... | collective-permute-start | bytes 86024 | tf_op jit(solution)/shard_map/ppermute | solution.py:574
  7.9 4.2 %collective-permute-start.4 = (f32[24,128]{1,0:T(8,128)S(1)}, f32[24,128]{1,0:T(8,128)S(1)}, u32[]{:S(2)}, u32[]{:S(2)}) collective-permute-start(f32[24,128]{1,0:T(8,128)S(1)} %get-tuple-element.29), channel_id=1, source_target_pairs={{0,1},{1,0},{2,3},{3,2},{4,5},{5,4},{6,7},{7,6},{8,9},{9,8},{10,11... | collective-permute-start | bytes 36872 | tf_op jit(solution)/shard_map/ppermute | solution.py:574
  8.1 4.5 %collective-permute-start.3 = (f32[8,128]{1,0:T(8,128)S(1)}, f32[8,128]{1,0:T(8,128)S(1)}, u32[]{:S(2)}, u32[]{:S(2)}) collective-permute-start(f32[8,128]{1,0:T(8,128)S(1)} %get-tuple-element.23.refs_10_), channel_id=1, source_target_pairs={{0,3},{1,2},{2,1},{3,0},{4,7},{5,6},{6,5},{7,4},{8,11},{9,10},{10,... | collective-permute-start | bytes 12296 | tf_op jit(solution)/shard_map/ppermute | solution.py:574
  11.0 1.5 %collective-permute-start.2 = (f32[8,128]{1,0:T(8,128)S(1)}, f32[8,128]{1,0:T(8,128)S(1)}, u32[]{:S(2)}, u32[]{:S(2)}) collective-permute-start(f32[8,128]{1,0:T(8,128)S(1)} %get-tuple-element.22), channel_id=1, source_target_pairs={{0,1},{1,0},{2,3},{3,2},{4,5},{5,4},{6,7},{7,6},{8,9},{9,8},{10,11... | collective-permute-start | bytes 12296 | tf_op jit(solution)/shard_map/ppermute | solution.py:574
